TPU v7x, 128 devices: a whole 4x4x4 slice. The times are simulated.
128 devices in a mesh: atom: 16 (over x_hi, y, core), mode: 8 (over x_lo, z).
Axes of the slice: x: 4 (x_hi: 2, x_lo: 2; x = x_hi * 2 + x_lo), y: 4, z: 4, core: 2. Of those that a mesh axis runs over, the one named last changes fastest.
Arguments:
- features: float32 [128, 16384], P(None, 'atom'), may hold values from -6 to 6
- positions: float32 [3, 16384], P(None, 'atom'), may hold values from 0 to 1, as said below
- wavevectors: int32 [3, 8192], P(None, 'mode'), may hold values from -768 to 768, as said below
- mode_filter: float32 [128, 8192], P(None, 'mode'), may hold values from -12 to 12
- radial_mix: float32 [4, 128, 128], replicated, may hold values from -0.03125 to 0.03125
- radial_rates: float32 [4], replicated, may hold values from 0.2 to 3
- neighbour_ids: int32 [128, 5], P(('atom', 'mode')), may hold values from 0 to 127, as said below
- live_counts: int32 [128], P(('atom', 'mode')), may hold values from 1 to 5, as said below
- cotangent: float32 [128, 16384], P(None, ('atom', 'mode')), may hold values from -6 to 6
Outputs:
- layer_out: float32 [128, 16384], P(None, ('atom', 'mode'))
- grad_features: float32 [128, 16384], P(None, ('atom', 'mode'))
- grad_filter: float32 [128, 8192], P(None, 'mode')
Inputs may be any that keep to these rules, and one draw needn't show every extreme that they name: `positions`: row 0 of atom i lies between b / 128 and (b + 1) / 128, with b = i // 128; rows 1 and 2 lie anywhere in the range. `wavevectors`: row 0 lies between -768 and 768; rows 1 and 2 lie between -12 and 12. `neighbour_ids`: row b lists the 5 blocks (b + o) mod 128, o from -2 to 2, each once, in some order; only the first live_counts[b] slots are live. `live_counts`: some block has all 5 slots live.
All inputs are finite; a program needn't handle non-finite values.
Results may differ from a plain program's by a relative error of at most 0.00035.
Values sent between devices are 32-bit elements; how exact they have to be, the bound alone decides.
No kernel may reach another device: no remote copies, remote signals or barrier semaphores. Data moves between devices by JAX's collectives and lax.ppermute only.
A program may use at most 64 MiB of HBM per device.

v0:
```python
import jax
import jax.numpy as jnp
from jax import lax
from jax.experimental import pallas as pl
from jax.experimental.pallas import tpu as pltpu
from jax.sharding import PartitionSpec as P


BLOCK = 128
REACH = 2
SLOTS = 5
C = 128
ATOMS = 1024
MODES = 1024
HALF = 512
SHARE = 64
RADIAL = 4
ATOM_DEV = 16
MODE_DEV = 8
HALO_ROWS = 272

F32 = jnp.float32
BF16 = jnp.bfloat16
MAGIC = 12582912.0
LIMIT = 24 * 1024 * 1024
VMEM = pltpu.VMEM

NT = (((1,), (1,)), ((), ()))
NN = (((1,), (0,)), ((), ()))


def dot(a, b, dims):
    return lax.dot_general(a, b, dims, preferred_element_type=F32)


def pieces(x):
    high = x.astype(BF16)
    low = (x - high.astype(F32)).astype(BF16)
    return high, low


def cos_sin_turns(t):
    r = t - ((t + MAGIC) - MAGIC)
    y = r * r
    s = r * (4.44287957 + y * (-7.30781668 + y * (3.59777418 + y * -0.79119939)))
    c = 1.4142135 + y * (
        -6.97885095 + y * (5.73946038 + y * (-1.88355791 + y * 0.31068803))
    )
    return 1.0 - s * s, s * c


ROWS = 32
TILE = 256
CHUNK = 4 * TILE
TILES = HALF // TILE


def columns_of(rows):
    rows = list(rows)
    rows = rows + [rows[0]] * (8 - len(rows))
    eight = jnp.concatenate(rows, axis=0)
    return jnp.concatenate([eight] * (BLOCK // 8), axis=0).T


def tables_tile(pos_ref, wave_ref, tab_ref, first, tile, leave):
    shard = lax.axis_index("atom")
    mid = (2 * shard + 1).astype(F32) * (1.0 / 32.0)
    for group in range(TILE // BLOCK):
        at = tile * TILE + group * BLOCK
        w = wave_ref[:, pl.ds(pl.multiple_of(first + at, BLOCK), BLOCK)]
        start = ((w[0:1] * (2 * shard + 1)) & 31).astype(F32) * (1.0 / 32.0)
        wf = w.astype(F32)
        columns = columns_of((wf[0:1], wf[1:2], wf[2:3], start))
        for chunk in range(BLOCK // ROWS):
            part = columns[chunk * ROWS : (chunk + 1) * ROWS]
            w0, w1, w2, c0 = (
                jnp.broadcast_to(part[:, d : d + 1], (ROWS, BLOCK)) for d in range(4)
            )
            row = tile * CHUNK + group * BLOCK + chunk * ROWS
            for k in range(ATOMS // BLOCK):
                lanes = pl.ds(k * BLOCK, BLOCK)
                p0 = pos_ref[0:1, lanes] - mid
                p1 = pos_ref[1:2, lanes]
                p2 = pos_ref[2:3, lanes]
                t = w0 * p0 + (w1 * p1 + (w2 * p2 + c0))
                cos, sin = cos_sin_turns(t)
                ch, cl = pieces(cos)
                sh, sl = pieces(sin)
                tab_ref[row : row + ROWS, lanes] = ch
                tab_ref[TILE + row : TILE + row + ROWS, lanes] = sh
                tab_ref[2 * TILE + row : 2 * TILE + row + ROWS, lanes] = cl
                tab_ref[3 * TILE + row : 3 * TILE + row + ROWS, lanes] = sl
        leave(tile * CHUNK + group * BLOCK)


def sums_tile(tab_ref, rhs_ref, out_ref, tile, wide, copies=()):
    at = tile * CHUNK
    for copy in copies:
        copy.wait()
    both = dot(tab_ref[at : at + 2 * TILE, :], rhs_ref[...], NT)
    rest = dot(tab_ref[at + 2 * TILE : at + CHUNK, :], rhs_ref[0:wide, :], NT)
    total = both[:, :wide] + both[:, wide:] + rest
    for trig in range(2):
        out_ref[tile * TILE : (tile + 1) * TILE, trig * wide : (trig + 1) * wide] = (
            total[trig * TILE : (trig + 1) * TILE]
        )


def cot_rows(cot_ref, rhs_ref, high_at, low_at):
    for k in range(MODE_DEV):
        high, low = pieces(cot_ref[k, 0:C, :])
        rhs_ref[high_at : high_at + C, k * BLOCK : (k + 1) * BLOCK] = high
        rhs_ref[low_at : low_at + C, k * BLOCK : (k + 1) * BLOCK] = low


def tables_kernel(own, feat_hbm, pos_ref, wave_ref, dep_ref, *rest):
    out_ref, tab_hbm, rhs_ref, tab_ref, feat_ref, sems = rest
    fetch = pltpu.make_async_copy(feat_hbm, feat_ref, sems.at[0])
    fetch.start()
    core = lax.axis_index("atom") % 2
    first = HALF * (core if own else 1 - core)
    copies = []

    def leave(row):
        for kind in range(4):
            rows = pl.ds(row + kind * TILE, BLOCK)
            sem = sems.at[1 + len(copies)]
            copies.append(
                pltpu.make_async_copy(tab_ref.at[rows], tab_hbm.at[rows], sem)
            )
            copies[-1].start()

    for tile in range(TILES):
        tables_tile(pos_ref, wave_ref, tab_ref, first, tile, leave)
        if tile == 0:
            fetch.wait()
            high, low = pieces(feat_ref[...])
            rhs_ref[0:C, :] = high
            rhs_ref[C:, :] = low
        sums_tile(tab_ref, rhs_ref, out_ref, tile, C)
    for copy in copies:
        copy.wait()


def spec():
    return pl.BlockSpec(memory_space=VMEM)


def call(body, ins, outs, scratch=(), flops=10**8, smem=(), far=(), far_outs=(), plain=(), args_in=(), any_in=()):
    args, in_specs = [], []
    for k, x in enumerate(ins):
        if k in smem:
            in_specs.append(pl.BlockSpec(memory_space=pltpu.SMEM))
        elif k in any_in:
            in_specs.append(pl.BlockSpec(memory_space=pl.ANY))
        elif k in far:
            in_specs.append(pl.BlockSpec(memory_space=pltpu.HBM))
            x = pltpu.with_memory_space_constraint(x, pltpu.HBM)
        else:
            in_specs.append(spec())
            if k not in args_in:
                x = pltpu.with_memory_space_constraint(x, VMEM)
        args.append(x)
    size = sum(x.size * x.dtype.itemsize for x in ins)
    return pl.pallas_call(
        body,
        out_shape=tuple(
            pltpu.HBM(shape, kind)
            if k in far_outs
            else (jax.ShapeDtypeStruct if k in plain else VMEM)(shape, kind)
            for k, (shape, kind) in enumerate(outs)
        ),
        in_specs=in_specs,
        out_specs=tuple(
            pl.BlockSpec(memory_space=pltpu.HBM) if k in far_outs else spec()
            for k in range(len(outs))
        ),
        scratch_shapes=list(scratch),
        compiler_params=pltpu.CompilerParams(vmem_limit_bytes=LIMIT),
        cost_estimate=pl.CostEstimate(
            flops=flops, bytes_accessed=size, transcendentals=0
        ),
    )(*args)


def tables_call(own, feat, pos, wave, dep):
    def body(*refs):
        tables_kernel(own, *refs)

    return call(
        body,
        (feat, pos, wave, dep),
        (((HALF, 2 * C), F32), ((4 * HALF, ATOMS), BF16)),
        [
            VMEM((2 * C, ATOMS), BF16),
            VMEM((4 * HALF, ATOMS), BF16),
            VMEM((C, ATOMS), F32),
            pltpu.SemaphoreType.DMA((1 + 4 * HALF // BLOCK,)),
        ],
        4 * 10**9,
        far=(0, 3),
        far_outs=(1,),
    )


def fetched(tab_hbm, tab_ref, sems, tiles):
    copies = []
    for tile in tiles:
        rows = pl.ds(tile * CHUNK, CHUNK)
        copy = pltpu.make_async_copy(tab_hbm.at[rows], tab_ref.at[rows], sems.at[tile])
        copy.start()
        copies.append(copy)
    return copies


def ahead(next_hbm, next_ref, sem):
    copy = pltpu.make_async_copy(next_hbm.at[pl.ds(0, CHUNK)], next_ref, sem)
    copy.start()
    return copy


def cot_kernel(first, cot_ref, tab_hbm, other_ref, *rest):
    if first:
        feat_hbm, pos_hbm, out_ref, next_ref, rim_ref, rhs_ref, tab_ref, sems, pos_ref = rest
        copies = fetched(tab_hbm, tab_ref, sems, range(TILES))
        pad = REACH * BLOCK
        tail = lax.axis_index("mode") < MODE_DEV // 2
        block = jnp.where(tail, MODE_DEV - REACH, 0)
        lanes = pl.ds(pl.multiple_of(block * BLOCK, BLOCK), pad)
        later = [
            pltpu.make_async_copy(pos_hbm, pos_ref, sems.at[TILES + 1]),
            pltpu.make_async_copy(
                feat_hbm.at[:, lanes], rim_ref.at[pl.ds(0, C)], sems.at[TILES + 2]
            ),
        ]
        for copy in later:
            copy.start()
        later.append(ahead(other_ref, next_ref, sems.at[TILES]))
        for k in range(REACH):
            rim_ref[C + 8 :, k * BLOCK : (k + 1) * BLOCK] = cot_ref[block + k]
        rim_ref[C : C + 8, :] = jnp.zeros((8, pad), F32)
    else:
        out_ref, rhs_ref, tab_ref, sems = rest
        copies = [None] + fetched(tab_hbm, tab_ref, sems, range(1, TILES))
    cot_rows(cot_ref, rhs_ref, 0, C)
    for tile in range(TILES):
        if copies[tile] is None:
            sums_tile(other_ref, rhs_ref, out_ref, tile, C)
        else:
            copies[tile].wait()
            sums_tile(tab_ref, rhs_ref, out_ref, tile, C)
    if first:
        for copy in later:
            copy.wait()
        rim_ref[C : C + 3, :] = pos_ref[:, lanes]


def cot_call(first, cot, tab, other, *more):
    def body(*refs):
        cot_kernel(first, *refs)

    outs = [((HALF, 2 * C), F32)]
    scratch = [
        VMEM((2 * C, ATOMS), BF16),
        VMEM((4 * HALF, ATOMS), BF16),
        pltpu.SemaphoreType.DMA((TILES + 3,)),
    ]
    if first:
        outs += [((CHUNK, ATOMS), BF16), ((HALO_ROWS, REACH * BLOCK), F32)]
        scratch.append(VMEM((3, ATOMS), F32))
    return call(
        body,
        (cot, tab, other, *more),
        outs,
        scratch,
        2 * 10**9,
        far=(1, 2, 3, 4) if first else (1,),
    )


def merge_kernel(feat_ref, cot_ref, feat_got_ref, cot_got_ref, out_ref):
    for k in range(8):
        rows = slice(k * SHARE, (k + 1) * SHARE)
        for trig in range(2):
            for part in range(2):
                lanes = slice((2 * trig + part) * C, (2 * trig + part + 1) * C)
                here = slice(trig * C, (trig + 1) * C)
                own = (feat_ref, cot_ref)[part]
                got = (feat_got_ref, cot_got_ref)[part]
                out_ref[k, :, lanes] = own[rows, here] + got[rows, here]


def give_back_kernel(own, sums_ref, filt_hbm, tab_hbm, other_ref, *rest):
    if own:
        acc_ref, next_ref, lhs_ref, tab_ref, filt_ref, sems = rest
    else:
        acc_ref, out_hbm, lhs_ref, tab_ref, filt_ref, sems, out_ref = rest
    core = lax.axis_index("atom") % 2
    at = pl.multiple_of(HALF * (core if own else 1 - core), HALF)
    fetch = pltpu.make_async_copy(
        filt_hbm.at[:, pl.ds(at, HALF)], filt_ref, sems.at[TILES]
    )
    fetch.start()
    if own:
        copies = fetched(tab_hbm, tab_ref, sems, range(TILES))
        later = ahead(other_ref, next_ref, sems.at[TILES + 1])
    else:
        copies = [None] + fetched(tab_hbm, tab_ref, sems, range(1, TILES))
    fetch.wait()
    scale = 1.0 / (ATOM_DEV * ATOMS)
    for k in range(HALF // C):
        filt = filt_ref[:, k * C : (k + 1) * C] * scale
        tile, part = divmod(k * C, TILE)
        for trig in range(2):
            lanes = pl.ds((tile * 2 + trig) * TILE + part, C)
            for row in range(2):
                sums = sums_ref[k * C : (k + 1) * C, pl.ds((2 * trig + row) * C, C)]
                high, low = pieces(filt * sums.T)
                lhs_ref[row * C : (row + 1) * C, lanes] = high
                lhs_ref[(2 + row) * C : (3 + row) * C, lanes] = low
    width = 2 * BLOCK
    stores = []
    for n in range(TILES):
        if copies[n] is not None:
            copies[n].wait()
        table = other_ref if copies[n] is None else tab_ref
        depth = slice(n * 2 * TILE, (n + 1) * 2 * TILE)
        for k in range(ATOMS // width):
            lanes = slice(k * width, (k + 1) * width)
            top = n * CHUNK
            both = dot(lhs_ref[:, depth], table[top : top + 2 * TILE, lanes], NN)
            more = dot(
                lhs_ref[0 : 2 * C, depth],
                table[top + 2 * TILE : top + CHUNK, lanes],
                NN,
            )
            part = both[: 2 * C] + both[2 * C :] + more
            if not own and n == 0:
                part = part + acc_ref[:, lanes]
            if own and n == 0:
                acc_ref[:, lanes] = part
            elif own:
                acc_ref[:, lanes] = acc_ref[:, lanes] + part
            else:
                for side in range(2):
                    half = part[:, side * BLOCK : (side + 1) * BLOCK]
                    if n:
                        half = half + out_ref[2 * k + side]
                    out_ref[2 * k + side] = half
                if n == TILES - 1:
                    pair = pl.ds(2 * k, 2)
                    stores.append(
                        pltpu.make_async_copy(
                            out_ref.at[pair], out_hbm.at[pair], sems.at[TILES + 2 + k]
                        )
                    )
                    stores[-1].start()
    for store in stores:
        store.wait()
    if own:
        later.wait()


def give_back_call(own, sums, filt, tab, other, acc=None):
    def body(*refs):
        give_back_kernel(own, *refs)

    args = [sums, filt, tab, other]
    if own:
        outs = [((2 * C, ATOMS), F32), ((CHUNK, ATOMS), BF16)]
    else:
        args.append(acc)
        outs = [((MODE_DEV, 2 * C, BLOCK), F32)]
    return call(
        body,
        args,
        outs,
        [
            VMEM((4 * C, 2 * HALF), BF16),
            VMEM((4 * HALF, ATOMS), BF16),
            VMEM((C, HALF), F32),
            pltpu.SemaphoreType.DMA((TILES + 2 + ATOMS // (2 * BLOCK),)),
        ]
        + ([] if own else [VMEM(outs[0][0], F32)]),
        4 * 10**9,
        far=(1, 2, 3) if own else (1, 2),
        far_outs=() if own else (0,),
    )


def grad_kernel(own_ref, oth_ref, grad_ref):
    core = lax.axis_index("atom") % 2
    scale = 1.0 / (ATOM_DEV * ATOMS)
    for half in range(2):
        ref = (own_ref, oth_ref)[half]
        at = pl.multiple_of(HALF * (core if half == 0 else 1 - core), HALF)
        for k in range(HALF // C):
            rows = slice(k * C, (k + 1) * C)
            grad = (
                ref[rows, 0:C] * ref[rows, C : 2 * C]
                + ref[rows, 2 * C : 3 * C] * ref[rows, 3 * C :]
            )
            grad_ref[:, pl.ds(pl.multiple_of(at + k * C, C), C)] = grad.T * scale


def near_kernel(
    rim_ref,
    feat_ref,
    pos_ref,
    cot_ref,
    mix_hbm,
    rate_ref,
    out_ref,
    back_ref,
    ext_ref,
    rhs_ref,
    mix_ref,
    pos_vmem,
    sems,
):
    own = lax.axis_index("mode")
    pad = REACH * BLOCK
    middle = pl.ds(pad, ATOMS)
    rim_at = jnp.where(own < MODE_DEV // 2, 0, pad + ATOMS)
    moves = [
        (pos_ref, pos_vmem),
        (rim_ref, ext_ref.at[:, pl.ds(pl.multiple_of(rim_at, BLOCK), pad)]),
        (feat_ref, ext_ref.at[pl.ds(0, C), middle]),
        (mix_hbm, mix_ref),
    ]
    for k in range(MODE_DEV):
        lanes = pl.ds(pad + k * BLOCK, BLOCK)
        moves.append((cot_ref.at[k], ext_ref.at[pl.ds(C + 8, C + 8), lanes]))
    copies = [
        pltpu.make_async_copy(src, dst, sems.at[k]) for k, (src, dst) in enumerate(moves)
    ]
    for copy in copies:
        copy.start()
    for copy in copies:
        copy.wait()
    ext_ref[C : C + 3, pad : pad + ATOMS] = pos_vmem[...]
    shard = lax.axis_index("atom")
    total_blocks = ATOM_DEV * MODE_DEV

    def unit(block, row):
        return row * float(total_blocks) - block.astype(F32)

    def halves(row):
        q = row - 0.5
        y = q * q
        s = q * (
            3.14159265
            + y
            * (-5.16771276 + y * (2.55016332 + y * (-0.5992522 + y * (0.0820504 - 0.00702839 * y))))
        )
        c = 1.0 + y * (
            -4.93480214
            + y * (4.05870916 + y * (-1.335212 + y * (0.23493731 - 0.02439632 * y)))
        )
        return -s, c

    me = shard * MODE_DEV + own
    here = ext_ref[C : C + 8, pl.ds(pl.multiple_of(pad + own * BLOCK, BLOCK), BLOCK)]
    u_own = unit(me, here[0:1])
    c1, s1 = halves(here[1:2])
    c2, s2 = halves(here[2:3])
    columns = columns_of((u_own, c1, s1, c2, s2))
    wide = [jnp.broadcast_to(columns[:, k : k + 1], (BLOCK, BLOCK)) for k in range(5)]
    span = 2 * REACH + 1
    dist = []
    live = ext_ref[264:265, pl.ds(pl.multiple_of(pad + own * BLOCK, BLOCK), BLOCK)]
    for o in range(span):
        at = pl.ds(pl.multiple_of((own + o) * BLOCK, BLOCK), BLOCK)
        block = ext_ref[:, at]
        there = lax.rem(me + o - REACH + total_blocks, total_blocks)
        near = block[C : C + 8]
        x = wide[0] - (unit(there, near[0:1]) + float(o - REACH))
        d1c, d1s = halves(near[1:2])
        d2c, d2s = halves(near[2:3])
        y = x * x
        z = y * (3.14159265 / total_blocks) ** 2
        d = y * (1.0 + z * (-1.0 / 3.0 + z * (2.0 / 45.0)))
        e1 = wide[2] * d1c - wide[1] * d1s
        e2 = wide[4] * d2c - wide[3] * d2s
        d = d + (e1 * e1 + e2 * e2) * (2.0 / 3.14159265) ** 2
        dist.append(d)
        lanes = slice(o * BLOCK, (o + 1) * BLOCK)
        high, low = pieces(block[0:C] * live[0:1, o : o + 1])
        rhs_ref[0:C, lanes] = high
        rhs_ref[2 * C : 3 * C, lanes] = low
        lists_me = block[264:265, span - 1 - o : span - o]
        high, low = pieces(block[136 : 136 + C] * lists_me)
        rhs_ref[C : 2 * C, lanes] = high
        rhs_ref[3 * C :, lanes] = low
    out = ext_ref[0:C, pl.ds(pl.multiple_of(pad + own * BLOCK, BLOCK), BLOCK)]
    back = ext_ref[136 : 136 + C, pl.ds(pl.multiple_of(pad + own * BLOCK, BLOCK), BLOCK)]
    for r in range(RADIAL):
        rate = rate_ref[r]
        highs, lows = [], []
        for o in range(span):
            high, low = pieces(jnp.exp(dist[o] * -rate))
            highs.append(high)
            lows.append(low)
        weights_high = jnp.concatenate(highs, axis=1)
        weights_low = jnp.concatenate(lows, axis=1)
        both = dot(rhs_ref[...], weights_high, NT)
        got = (
            both[: 2 * C]
            + both[2 * C :]
            + dot(rhs_ref[0 : 2 * C, :], weights_low, NT)
        )
        high, low = pieces(got)
        mix = mix_ref[r]
        mh, ml = pieces(mix)
        th, tl = pieces(mix.T)
        out = out + (
            dot(th, high[:C], NN) + dot(th, low[:C], NN) + dot(tl, high[:C], NN)
        )
        back = back + (
            dot(mh, high[C:], NN) + dot(mh, low[C:], NN) + dot(ml, high[C:], NN)
        )
    out_ref[...] = out
    back_ref[...] = back


def near_call(rim, feat, pos, cot, mix, rates):
    return call(
        near_kernel,
        (rim, feat, pos, cot, mix, rates),
        (((C, BLOCK), F32), ((C, BLOCK), F32)),
        [
            VMEM((HALO_ROWS, ATOMS + 2 * REACH * BLOCK), F32),
            VMEM((4 * C, (2 * REACH + 1) * BLOCK), BF16),
            VMEM((RADIAL, C, C), F32),
            VMEM((3, ATOMS), F32),
            pltpu.SemaphoreType.DMA((4 + MODE_DEV,)),
        ],
        2 * 10**9,
        smem=(5,),
        any_in=(0, 1, 2, 3, 4),
    )


def pack_kernel(ids_hbm, live_ref, cot_hbm, pos_hbm, wave_hbm, *rest):
    out_hbm, pos_ref, wave_ref, ids_ref, pack_ref, sems = rest
    fetches = [
        pltpu.make_async_copy(cot_hbm, pack_ref.at[pl.ds(0, C)], sems.at[MODE_DEV]),
        pltpu.make_async_copy(ids_hbm, ids_ref, sems.at[MODE_DEV + 1]),
        pltpu.make_async_copy(pos_hbm, pos_ref, sems.at[MODE_DEV + 2]),
        pltpu.make_async_copy(wave_hbm, wave_ref, sems.at[MODE_DEV + 3]),
    ]
    for fetch in fetches:
        fetch.start()
    total_blocks = ATOM_DEV * MODE_DEV
    me = lax.axis_index("atom") * MODE_DEV + lax.axis_index("mode")
    lane = lax.broadcasted_iota(jnp.int32, (8, BLOCK), 1)
    live = jnp.zeros((8, BLOCK), F32)
    fetches[1].wait()
    for slot in range(SLOTS):
        offset = lax.rem(ids_ref[0, slot] - me + REACH + total_blocks, total_blocks)
        offset = jnp.where(slot < live_ref[0], offset, BLOCK)
        live = jnp.where(lane == offset, 1.0, live)
    pack_ref[C:, :] = live
    fetches[0].wait()
    copies = [
        pltpu.make_async_copy(pack_ref, out_hbm.at[k], sems.at[k]) for k in range(MODE_DEV)
    ]
    for copy in copies:
        copy.start()
    for copy in copies + fetches[2:]:
        copy.wait()


def share_kernel(parts_ref, out_ref):
    share = parts_ref[0]
    for k in range(1, ATOM_DEV // 2):
        share = share + parts_ref[k]
    for k in range(ATOM_DEV // 2):
        out_ref[k] = share


def finish_kernel(near_ref, back_ref, parts_ref, out_ref, grad_ref):
    out = near_ref[...]
    grad = back_ref[...]
    for k in range(MODE_DEV):
        out = out + parts_ref[k, 0:C]
        grad = grad + parts_ref[k, C:]
    out_ref[...] = out
    grad_ref[...] = grad


def per_device(
    features,
    positions,
    wavevectors,
    mode_filter,
    radial_mix,
    radial_rates,
    neighbour_ids,
    live_counts,
    cotangent,
):
    core_swap = [(i, i ^ 1) for i in range(ATOM_DEV)]
    chips = [[c + 2 * i for i in range(ATOM_DEV // 2)] for c in range(2)]
    rims = []
    for i in range(ATOM_DEV):
        for m in range(REACH):
            after = (i + 1) % ATOM_DEV
            rims.append((i * MODE_DEV + m, after * MODE_DEV + m))
            last = MODE_DEV - 1 - m
            rims.append((after * MODE_DEV + last, i * MODE_DEV + last))

    def exchange(x):
        return lax.all_to_all(x, "atom", 0, 0, axis_index_groups=chips, tiled=True)

    packed, pos_near, wave_near = call(
        pack_kernel,
        (neighbour_ids, live_counts, cotangent, positions, wavevectors),
        (
            ((MODE_DEV, C + 8, BLOCK), F32),
            (positions.shape, F32),
            (wavevectors.shape, jnp.int32),
        ),
        [
            pltpu.SMEM((1, SLOTS), jnp.int32),
            VMEM((C + 8, BLOCK), F32),
            pltpu.SemaphoreType.DMA((MODE_DEV + 4,)),
        ],
        smem=(1,),
        far=(0, 2, 3, 4),
        far_outs=(0,),
    )
    cot = lax.all_to_all(packed, "mode", 0, 0, tiled=True)

    f_own, tab_own = tables_call(True, features, pos_near, wave_near, packed)
    f_oth, tab_oth = tables_call(False, features, pos_near, wave_near, tab_own)
    f_got = lax.ppermute(f_oth, "atom", core_swap)
    cot, f_oth = lax.optimization_barrier((cot, f_oth))
    c_oth, tab_next, rim = cot_call(True, cot, tab_oth, tab_own, features, positions)
    rim = lax.ppermute(rim, ("atom", "mode"), rims)
    c_got = lax.ppermute(c_oth, "atom", core_swap)
    cot, c_oth = lax.optimization_barrier((cot, c_oth))
    (c_own,) = cot_call(False, cot, tab_own, tab_next)
    (parts,) = call(
        merge_kernel, (f_own, c_own, f_got, c_got), (((8, SHARE, 4 * C), F32),)
    )
    parts = exchange(parts)
    (share,) = call(share_kernel, (parts,), ((parts.shape, F32),))
    own = exchange(share).reshape(HALF, 4 * C)
    oth = lax.ppermute(own, "atom", core_swap)
    acc, tab_next = give_back_call(True, own, mode_filter, tab_own, tab_oth)
    (back,) = give_back_call(False, oth, mode_filter, tab_oth, tab_next, acc)
    back, cot, rim = lax.optimization_barrier((back, cot, rim))
    near_out, near_back = near_call(
        rim, features, positions, cot, radial_mix, radial_rates
    )
    back = lax.all_to_all(back, "mode", 0, 0, tiled=True)
    (grad_filter,) = call(
        grad_kernel, (own, oth), (((C, MODES), F32),), plain=(0,), args_in=(0, 1)
    )
    layer_out, grad_features = call(
        finish_kernel,
        (near_out, near_back, back),
        (((C, BLOCK), F32), ((C, BLOCK), F32)),
        plain=(0, 1),
        args_in=(0, 1),
    )
    return (layer_out, grad_features, grad_filter)


def solution(mesh):
    in_specs = (
        P(None, "atom"),
        P(None, "atom"),
        P(None, "mode"),
        P(None, "mode"),
        P(),
        P(),
        P(("atom", "mode"), None),
        P(("atom", "mode")),
        P(None, ("atom", "mode")),
    )
    out_specs = (P(None, ("atom", "mode")), P(None, ("atom", "mode")), P(None, "mode"))
    return jax.shard_map(
        per_device, mesh=mesh, in_specs=in_specs, out_specs=out_specs, check_vma=False
    )
```

profile of v0, /device:TPU:0, one launch (start us, length us, event | category | flops | bytes accessed | tf_op | source)
XLA Modules:
  0.0 99.6 jit_solution(7282617342916518635)
XLA Ops:
  1.3 1.8 %shard_map.112 = (f32[8,136,128]{2,1,0:T(8,128)}, f32[3,1024]{1,0:T(4,128)S(1)}, s32[3,1024]{1,0:T(4,128)S(1)}) custom-call(s32[1,5]{1,0:T(1,128)} %ids_hbm.1, s32[1]{0:T(128)S(6)} %copy.12.live_ref, f32[128,128]{1,0:T(8,128)} %cot_hbm.1, f32[3,1024]{1,0:T(4,128)} %pos_ref.1, s32[3,1024]{1,0:T(4,128)} %wave_hbm.1), custom_call_target="tpu_custom_call" | custom-call | flops 100000000 | bytes 90136 | tf_op jit(solution)/shard_map/pallas_call | solution.py:165
  3.1 6.4 %all-to-all-start = ((f32[8,136,128]{2,1,0:T(8,128)}), f32[8,136,128]{2,1,0:T(8,128)S(1)}, u32[]{:S(2)}, u32[]{:S(2)}) async-start(f32[8,136,128]{2,1,0:T(8,128)} %get-tuple-element.26.refs_3_), calls=%async_computation | async-start | bytes 1114112 | tf_op jit(solution)/shard_map/all_to_all | solution.py:633
  9.5 4.5 %shard_map.113 = (f32[512,256]{1,0:T(8,128)S(1)}, bf16[2048,1024]{1,0:T(8,128)(2,1)}) custom-call(f32[128,1024]{1,0:T(8,128)} %feat_ref.1, f32[3,1024]{1,0:T(4,128)S(1)} %get-tuple-element.24.refs_1_, s32[3,1024]{1,0:T(4,128)S(1)} %get-tuple-element.25.refs_2_, f32[8,136,128]{2,1,0:T(8,128)} %get-tuple-element.26.refs_3_), custom_call_target="tpu_custom_call" | custom-call | flops 4000000000 | bytes 1105920 | tf_op jit(solution)/shard_map/pallas_call | solution.py:165
  14.0 4.5 %shard_map.114 = (f32[512,256]{1,0:T(8,128)S(1)}, bf16[2048,1024]{1,0:T(8,128)(2,1)}) custom-call(f32[128,1024]{1,0:T(8,128)} %feat_ref.1, f32[3,1024]{1,0:T(4,128)S(1)} %get-tuple-element.24.refs_1_, s32[3,1024]{1,0:T(4,128)S(1)} %get-tuple-element.25.refs_2_, bf16[2048,1024]{1,0:T(8,128)(2,1)} %get-tuple-element.28.refs_3_.refs_2_.refs_1_), custom_call_target="tpu_custom_call" | custom-call | flops 4000000000 | bytes 4743168 | tf_op jit(solution)/shard_map/pallas_call | solution.py:165
  18.5 0.1 collective-permute-start
  18.6 0.6 all-to-all-done.refs_0_.cot_ref
  19.2 3.1 %shard_map.115 = (f32[512,256]{1,0:T(8,128)S(1)}, bf16[1024,1024]{1,0:T(8,128)(2,1)S(1)}, f32[272,256]{1,0:T(8,128)S(1)}) custom-call(f32[8,136,128]{2,1,0:T(8,128)S(1)} %all-to-all-done.refs_0_.cot_ref, bf16[2048,1024]{1,0:T(8,128)(2,1)} %get-tuple-element.31.refs_1_.refs_3_.refs_2_, bf16[2048,1024]{1,0:T(8,128)(2,1)} %get-tuple-element.28.refs_3_.refs_2_.refs_1_, ...), custom_call_target="tpu_custom_call" | custom-call | flops 2000000000 | bytes 9482240 | tf_op jit(solution)/shard_map/pallas_call | solution.py:165
  22.4 0.1 collective-permute-start.1
  22.5 2.8 %shard_map.116.cot_ref = f32[512,256]{1,0:T(8,128)S(1)} custom-call(f32[8,136,128]{2,1,0:T(8,128)S(1)} %all-to-all-done.refs_0_.cot_ref, bf16[2048,1024]{1,0:T(8,128)(2,1)} %get-tuple-element.28.refs_3_.refs_2_.refs_1_, bf16[1024,1024]{1,0:T(8,128)(2,1)S(1)} %get-tuple-element.34.refs_2_), custom_call_target="tpu_custom_call" | custom-call | flops 2000000000 | bytes 6848512 | tf_op jit(solution)/shard_map/pallas_call | solution.py:165
  25.3 0.0 collective-permute-done.feat_got_ref
  25.3 0.0 collective-permute-done.1.cot_got_ref
  25.3 0.1 shard_map.117
  25.4 24.1 %all_to_all.20.parts_ref = f32[8,64,512]{2,1,0:T(8,128)S(1)} all-to-all(f32[8,64,512]{2,1,0:T(8,128)S(1)} %shard_map.117), channel_id=1, replica_groups={{0,16,32,48,64,80,96,112},{8,24,40,56,72,88,104,120},{1,17,33,49,65,81,..., dimensions={0} | all-to-all | bytes 2097152 | tf_op jit(solution)/shard_map/all_to_all | solution.py:614
  49.5 0.1 shard_map.118
  49.6 20.1 %all_to_all.21 = f32[8,64,512]{2,1,0:T(8,128)S(1)} all-to-all(f32[8,64,512]{2,1,0:T(8,128)S(1)} %shard_map.118), channel_id=1, replica_groups={{0,16,32,48,64,80,96,112},{8,24,40,56,72,88,104,120},{1,17,33,49,65,81,..., dimensions={0} | all-to-all | bytes 2097152 | tf_op jit(solution)/shard_map/all_to_all | solution.py:614
  69.7 0.0 collective-permute-start.2
  69.7 2.4 %collective-permute-start.3 = (f32[272,256]{1,0:T(8,128)S(1)}, f32[272,256]{1,0:T(8,128)S(1)}, u32[]{:S(2)}, u32[]{:S(2)}) collective-permute-start(f32[272,256]{1,0:T(8,128)S(1)} %get-tuple-element.37), channel_id=1, source_target_pairs={{0,8},{15,7},{1,9},{14,6},{8,16},{23,15},{9,17},{22,14},{16,24},{3... | collective-permute-start | bytes 835592 | tf_op jit(solution)/shard_map/ppermute | solution.py:640
  72.1 3.6 %shard_map.119 = (f32[256,1024]{1,0:T(8,128)S(1)}, bf16[1024,1024]{1,0:T(8,128)(2,1)S(1)}) custom-call(f32[512,512]{1,0:T(8,128)S(1)} %bitcast.2, f32[128,1024]{1,0:T(8,128)} %refs_1_.3, bf16[2048,1024]{1,0:T(8,128)(2,1)} %get-tuple-element.28.refs_3_.refs_2_.refs_1_, bf16[2048,1024]{1,0:T(8,128)(2,1)} %get-tuple-element.31.refs_1_.refs_3_.refs_2_), custom_call_target="tpu_custom_call" | custom-call | flops 4000000000 | bytes 9961472 | tf_op jit(solution)/shard_map/pallas_call | solution.py:165
  75.7 0.0 collective-permute-done.2.refs_0_.oth_ref
  75.7 0.0 copy-start
  75.7 4.1 %shard_map.120 = f32[8,256,128]{2,1,0:T(8,128)} custom-call(f32[512,512]{1,0:T(8,128)S(1)} %collective-permute-done.2.refs_0_.oth_ref, f32[128,1024]{1,0:T(8,128)} %refs_1_.3, bf16[2048,1024]{1,0:T(8,128)(2,1)} %get-tuple-element.31.refs_1_.refs_3_.refs_2_, bf16[1024,1024]{1,0:T(8,128)(2,1)S(1)} %get-tuple-element.35.refs_3_, ...), custom_call_target="tpu_custom_call" | custom-call | flops 4000000000 | bytes 8912896 | tf_op jit(solution)/shard_map/pallas_call | solution.py:165
  79.9 0.0 copy-done
  79.9 0.0 copy-start.2
  79.9 0.0 copy-start.3
  79.9 0.0 copy-start.5
  79.9 1.2 %collective-permute-done.3.rim_ref = f32[272,256]{1,0:T(8,128)S(1)} collective-permute-done((f32[272,256]{1,0:T(8,128)S(1)}, f32[272,256]{1,0:T(8,128)S(1)}, u32[]{:S(2)}, u32[]{:S(2)}) %collective-permute-start.3) | collective-permute-done | bytes 278560 | tf_op jit(solution)/shard_map/ppermute | solution.py:640
  81.1 3.9 %all-to-all-start.3 = ((f32[8,256,128]{2,1,0:T(8,128)}), f32[8,256,128]{2,1,0:T(8,128)S(1)}, u32[]{:S(2)}, u32[]{:S(2)}) async-start(f32[8,256,128]{2,1,0:T(8,128)} %shard_map.120), calls=%async_computation.3 | async-start | bytes 2097152 | tf_op jit(solution)/shard_map/all_to_all | solution.py:657
  85.1 0.0 copy-start.1
  85.1 1.2 %copy-done.1 = f32[512,512]{1,0:T(8,128)S(1)} copy-done((f32[512,512]{1,0:T(8,128)S(1)}, f32[512,512]{1,0:T(8,128)}, u32[]{:S(2)}) %copy-start.1) | copy-done | bytes 1048600
  86.3 1.0 %shard_map.123 = f32[128,1024]{1,0:T(8,128)} custom-call(f32[512,512]{1,0:T(8,128)S(1)} %bitcast.3, f32[512,512]{1,0:T(8,128)S(1)} %copy-done.1), custom_call_target="tpu_custom_call" | custom-call | flops 100000000 | bytes 2097152 | tf_op jit(solution)/shard_map/pallas_call | solution.py:165
  87.3 0.0 copy-done.2
  87.3 0.0 copy-done.3
  87.3 0.0 copy-done.5
  87.3 0.0 copy-start.4
  87.3 0.9 copy-done.4
  88.3 3.3 %shard_map.121 = (f32[128,128]{1,0:T(8,128)S(1)}, f32[128,128]{1,0:T(8,128)S(1)}) custom-call(f32[272,256]{1,0:T(8,128)S(1)} %collective-permute-done.3.rim_ref, f32[128,1024]{1,0:T(8,128)S(1)} %copy-done.2, f32[3,1024]{1,0:T(4,128)S(1)} %copy-done.3, f32[8,136,128]{2,1,0:T(8,128)S(1)} %all-to-all-done.refs_0_.cot_ref, f32[4,128,128]{2,1,0:T(8,128)S(1)} %copy-done.4, ...), custom_call_target="tpu_custom_call" | custom-call | flops 2000000000 | bytes 1634320 | tf_op jit(solution)/shard_map/pallas_call | solution.py:165
  91.5 7.4 %all-to-all-done.3.parts_ref = f32[8,256,128]{2,1,0:T(8,128)S(1)} async-done(((f32[8,256,128]{2,1,0:T(8,128)}), f32[8,256,128]{2,1,0:T(8,128)S(1)}, u32[]{:S(2)}, u32[]{:S(2)}) %all-to-all-start.3) | async-done | bytes 1048608 | tf_op jit(solution)/shard_map/all_to_all | solution.py:657
  98.9 0.7 shard_map.122
Async XLA Ops:
  3.1 16.1 %all-to-all-start = ((f32[8,136,128]{2,1,0:T(8,128)}), f32[8,136,128]{2,1,0:T(8,128)S(1)}, u32[]{:S(2)}, u32[]{:S(2)}) async-start(f32[8,136,128]{2,1,0:T(8,128)} %get-tuple-element.26.refs_3_), calls=%async_computation | async-start | bytes 1114112 | tf_op jit(solution)/shard_map/all_to_all | solution.py:633
  18.5 6.7 %collective-permute-start = (f32[512,256]{1,0:T(8,128)S(1)}, f32[512,256]{1,0:T(8,128)S(1)}, u32[]{:S(2)}, u32[]{:S(2)}) collective-permute-start(f32[512,256]{1,0:T(8,128)S(1)} %get-tuple-element.29), channel_id=1, source_target_pairs={{0,8},{8,0},{16,24},{24,16},{32,40},{40,32},{48,56},{56,48},{64,72... | collective-permute-start | bytes 1572872 | tf_op jit(solution)/shard_map/ppermute | solution.py:637
  22.4 2.9 %collective-permute-start.1 = (f32[512,256]{1,0:T(8,128)S(1)}, f32[512,256]{1,0:T(8,128)S(1)}, u32[]{:S(2)}, u32[]{:S(2)}) collective-permute-start(f32[512,256]{1,0:T(8,128)S(1)} %get-tuple-element.32), channel_id=1, source_target_pairs={{0,8},{8,0},{16,24},{24,16},{32,40},{40,32},{48,56},{56,48},{64,72... | collective-permute-start | bytes 1572872 | tf_op jit(solution)/shard_map/ppermute | solution.py:641
  69.7 6.0 %collective-permute-start.2 = (f32[512,512]{1,0:T(8,128)S(1)}, f32[512,512]{1,0:T(8,128)S(1)}, u32[]{:S(2)}, u32[]{:S(2)}) collective-permute-start(f32[512,512]{1,0:T(8,128)S(1)} %bitcast.1), channel_id=1, source_target_pairs={{0,8},{8,0},{16,24},{24,16},{32,40},{40,32},{48,56},{56,48},{64,72... | collective-permute-start | bytes 3145736 | tf_op jit(solution)/shard_map/ppermute | solution.py:650
  69.7 11.5 %collective-permute-start.3 = (f32[272,256]{1,0:T(8,128)S(1)}, f32[272,256]{1,0:T(8,128)S(1)}, u32[]{:S(2)}, u32[]{:S(2)}) collective-permute-start(f32[272,256]{1,0:T(8,128)S(1)} %get-tuple-element.37), channel_id=1, source_target_pairs={{0,8},{15,7},{1,9},{14,6},{8,16},{23,15},{9,17},{22,14},{16,24},{3... | collective-permute-start | bytes 835592 | tf_op jit(solution)/shard_map/ppermute | solution.py:640
  75.7 4.2 %copy-start = (f32[512,512]{1,0:T(8,128)}, f32[512,512]{1,0:T(8,128)S(1)}, u32[]{:S(2)}) copy-start(f32[512,512]{1,0:T(8,128)S(1)} %collective-permute-done.2.refs_0_.oth_ref) | copy-start | bytes 3145732
  79.9 7.4 %copy-start.2 = (f32[128,1024]{1,0:T(8,128)S(1)}, f32[128,1024]{1,0:T(8,128)}, u32[]{:S(2)}) copy-start(f32[128,1024]{1,0:T(8,128)} %feat_ref.1) | copy-start | bytes 1572868
  79.9 7.4 %copy-start.3 = (f32[3,1024]{1,0:T(4,128)S(1)}, f32[3,1024]{1,0:T(4,128)}, u32[]{:S(2)}) copy-start(f32[3,1024]{1,0:T(4,128)} %pos_ref.1) | copy-start | bytes 36868
  79.9 7.4 %copy-start.5 = (f32[4]{0:T(128)S(1)}, f32[4]{0:T(128)}, u32[]{:S(2)}) copy-start(f32[4]{0:T(128)} %rate_ref.1) | copy-start | bytes 52
  81.1 17.8 %all-to-all-start.3 = ((f32[8,256,128]{2,1,0:T(8,128)}), f32[8,256,128]{2,1,0:T(8,128)S(1)}, u32[]{:S(2)}, u32[]{:S(2)}) async-start(f32[8,256,128]{2,1,0:T(8,128)} %shard_map.120), calls=%async_computation.3 | async-start | bytes 2097152 | tf_op jit(solution)/shard_map/all_to_all | solution.py:657
  85.1 1.2 %copy-start.1 = (f32[512,512]{1,0:T(8,128)S(1)}, f32[512,512]{1,0:T(8,128)}, u32[]{:S(2)}) copy-start(f32[512,512]{1,0:T(8,128)} %copy-done) | copy-start | bytes 3145732
  87.3 1.0 copy-start.4
where the time goes:
time: 100 us; the launch traced here: 99.6 us
  blocking collectives  44.2 us (44%)
  Pallas kernels  29.7 us (30%)
  starting transfers between devices  12.9 us (13%)
  waiting for transfers between devices  9.23 us (9%)
  local copies, waits for them, and re-layouts  2.19 us (2%)
  between operations  1.46 us (1%)
    all_to_all x2, blocking collectives, exchange(): return lax.all_to_all(x, 'atom', 0, 0, axis_index_groups=chips, tiled=True)  44.2 us
    pallas_call x12, Pallas kernels, call(): pl.pallas_call(body, out_shape=tuple((pltpu.HBM(shape, kind) if k in far_...  29.7 us
    all_to_all x1, waiting for transfers between devices, per_device(): back = lax.all_to_all(back, 'mode', 0, 0, tiled=True)  7.4 us
    all_to_all x1, starting transfers between devices, per_device(): cot = lax.all_to_all(packed, 'mode', 0, 0, tiled=True)  6.36 us
    all_to_all x1, starting transfers between devices, per_device(): back = lax.all_to_all(back, 'mode', 0, 0, tiled=True)  3.93 us
    ppermute x1, starting transfers between devices, per_device(): rim = lax.ppermute(rim, ('atom', 'mode'), rims)  2.4 us
    unnamed x12, local copies, waits for them, and re-layouts  2.19 us
  transfers between devices with their start and end apart: 6, of which 3 were waited for; matrix products, arithmetic and copies ran while one was open for 0% of the time, Pallas kernels for 27%

commit v1 on v0

--- a/solution.py
+++ b/solution.py
@@ -292,24 +292,24 @@
 
 def give_back_kernel(own, sums_ref, filt_hbm, tab_hbm, other_ref, *rest):
     if own:
-        acc_ref, next_ref, lhs_ref, tab_ref, filt_ref, sems = rest
+        acc_ref, next_ref, filt_ref, lhs_ref, tab_ref, sems = rest
     else:
-        acc_ref, out_hbm, lhs_ref, tab_ref, filt_ref, sems, out_ref = rest
+        acc_ref, out_hbm, lhs_ref, tab_ref, sems, out_ref = rest
+        filt_ref = filt_hbm
     core = lax.axis_index("atom") % 2
     at = pl.multiple_of(HALF * (core if own else 1 - core), HALF)
-    fetch = pltpu.make_async_copy(
-        filt_hbm.at[:, pl.ds(at, HALF)], filt_ref, sems.at[TILES]
-    )
-    fetch.start()
     if own:
+        fetch = pltpu.make_async_copy(filt_hbm, filt_ref, sems.at[TILES])
+        fetch.start()
         copies = fetched(tab_hbm, tab_ref, sems, range(TILES))
         later = ahead(other_ref, next_ref, sems.at[TILES + 1])
     else:
         copies = [None] + fetched(tab_hbm, tab_ref, sems, range(1, TILES))
-    fetch.wait()
+    if own:
+        fetch.wait()
     scale = 1.0 / (ATOM_DEV * ATOMS)
     for k in range(HALF // C):
-        filt = filt_ref[:, k * C : (k + 1) * C] * scale
+        filt = filt_ref[:, pl.ds(pl.multiple_of(at + k * C, C), C)] * scale
         tile, part = divmod(k * C, TILE)
         for trig in range(2):
             lanes = pl.ds((tile * 2 + trig) * TILE + part, C)
@@ -367,7 +367,7 @@
 
     args = [sums, filt, tab, other]
     if own:
-        outs = [((2 * C, ATOMS), F32), ((CHUNK, ATOMS), BF16)]
+        outs = [((2 * C, ATOMS), F32), ((CHUNK, ATOMS), BF16), ((C, MODES), F32)]
     else:
         args.append(acc)
         outs = [((MODE_DEV, 2 * C, BLOCK), F32)]
@@ -378,12 +378,11 @@
         [
             VMEM((4 * C, 2 * HALF), BF16),
             VMEM((4 * HALF, ATOMS), BF16),
-            VMEM((C, HALF), F32),
             pltpu.SemaphoreType.DMA((TILES + 2 + ATOMS // (2 * BLOCK),)),
         ]
         + ([] if own else [VMEM(outs[0][0], F32)]),
         4 * 10**9,
-        far=(1, 2, 3) if own else (1, 2),
+        far=(1, 2, 3) if own else (2,),
         far_outs=() if own else (0,),
     )
 
@@ -648,8 +647,8 @@
     (share,) = call(share_kernel, (parts,), ((parts.shape, F32),))
     own = exchange(share).reshape(HALF, 4 * C)
     oth = lax.ppermute(own, "atom", core_swap)
-    acc, tab_next = give_back_call(True, own, mode_filter, tab_own, tab_oth)
-    (back,) = give_back_call(False, oth, mode_filter, tab_oth, tab_next, acc)
+    acc, tab_next, filt = give_back_call(True, own, mode_filter, tab_own, tab_oth)
+    (back,) = give_back_call(False, oth, filt, tab_oth, tab_next, acc)
     back, cot, rim = lax.optimization_barrier((back, cot, rim))
     near_out, near_back = near_call(
         rim, features, positions, cot, radial_mix, radial_rates

time: 100 us -> 100 us (level)
  no operation moved by 1% of the time
where the time goes in v1:
time: 100 us; the launch traced here: 99.4 us
  blocking collectives  44.2 us (44%)
  Pallas kernels  29.5 us (30%)
  starting transfers between devices  12.6 us (13%)
  waiting for transfers between devices  9.46 us (9%)
  local copies, waits for them, and re-layouts  2.19 us (2%)
  between operations  1.46 us (1%)
    all_to_all x2, blocking collectives, exchange(): return lax.all_to_all(x, 'atom', 0, 0, axis_index_groups=chips, tiled=True)  44.2 us
    pallas_call x12, Pallas kernels, call(): pl.pallas_call(body, out_shape=tuple((pltpu.HBM(shape, kind) if k in far_...  29.5 us
    all_to_all x1, waiting for transfers between devices, per_device(): back = lax.all_to_all(back, 'mode', 0, 0, tiled=True)  7.41 us
    all_to_all x1, starting transfers between devices, per_device(): cot = lax.all_to_all(packed, 'mode', 0, 0, tiled=True)  6.36 us
    all_to_all x1, starting transfers between devices, per_device(): back = lax.all_to_all(back, 'mode', 0, 0, tiled=True)  3.7 us
    ppermute x1, starting transfers between devices, per_device(): rim = lax.ppermute(rim, ('atom', 'mode'), rims)  2.4 us
    unnamed x12, local copies, waits for them, and re-layouts  2.19 us
  transfers between devices with their start and end apart: 6, of which 3 were waited for; matrix products, arithmetic and copies ran while one was open for 0% of the time, Pallas kernels for 27%

profile of v1, /device:TPU:0, one launch (start us, length us, event | category | flops | bytes accessed | tf_op | source)
XLA Modules:
  0.0 99.4 jit_solution(15746167159548572213)
XLA Ops:
  1.3 1.8 %shard_map.112 = (f32[8,136,128]{2,1,0:T(8,128)}, f32[3,1024]{1,0:T(4,128)S(1)}, s32[3,1024]{1,0:T(4,128)S(1)}) custom-call(s32[1,5]{1,0:T(1,128)} %ids_hbm.1, s32[1]{0:T(128)S(6)} %copy.12.live_ref, f32[128,128]{1,0:T(8,128)} %cot_hbm.1, f32[3,1024]{1,0:T(4,128)} %pos_ref.1, s32[3,1024]{1,0:T(4,128)} %wave_hbm.1), custom_call_target="tpu_custom_call" | custom-call | flops 100000000 | bytes 90136 | tf_op jit(solution)/shard_map/pallas_call | solution.py:165
  3.1 6.4 %all-to-all-start = ((f32[8,136,128]{2,1,0:T(8,128)}), f32[8,136,128]{2,1,0:T(8,128)S(1)}, u32[]{:S(2)}, u32[]{:S(2)}) async-start(f32[8,136,128]{2,1,0:T(8,128)} %get-tuple-element.27.refs_3_), calls=%async_computation | async-start | bytes 1114112 | tf_op jit(solution)/shard_map/all_to_all | solution.py:632
  9.5 4.5 %shard_map.113 = (f32[512,256]{1,0:T(8,128)S(1)}, bf16[2048,1024]{1,0:T(8,128)(2,1)}) custom-call(f32[128,1024]{1,0:T(8,128)} %feat_ref.1, f32[3,1024]{1,0:T(4,128)S(1)} %get-tuple-element.25.refs_1_, s32[3,1024]{1,0:T(4,128)S(1)} %get-tuple-element.26.refs_2_, f32[8,136,128]{2,1,0:T(8,128)} %get-tuple-element.27.refs_3_), custom_call_target="tpu_custom_call" | custom-call | flops 4000000000 | bytes 1105920 | tf_op jit(solution)/shard_map/pallas_call | solution.py:165
  14.0 4.5 %shard_map.114 = (f32[512,256]{1,0:T(8,128)S(1)}, bf16[2048,1024]{1,0:T(8,128)(2,1)}) custom-call(f32[128,1024]{1,0:T(8,128)} %feat_ref.1, f32[3,1024]{1,0:T(4,128)S(1)} %get-tuple-element.25.refs_1_, s32[3,1024]{1,0:T(4,128)S(1)} %get-tuple-element.26.refs_2_, bf16[2048,1024]{1,0:T(8,128)(2,1)} %get-tuple-element.29.refs_3_.refs_2_.refs_1_), custom_call_target="tpu_custom_call" | custom-call | flops 4000000000 | bytes 4743168 | tf_op jit(solution)/shard_map/pallas_call | solution.py:165
  18.5 0.1 collective-permute-start
  18.6 0.6 all-to-all-done.refs_0_.cot_ref
  19.2 3.1 %shard_map.115 = (f32[512,256]{1,0:T(8,128)S(1)}, bf16[1024,1024]{1,0:T(8,128)(2,1)S(1)}, f32[272,256]{1,0:T(8,128)S(1)}) custom-call(f32[8,136,128]{2,1,0:T(8,128)S(1)} %all-to-all-done.refs_0_.cot_ref, bf16[2048,1024]{1,0:T(8,128)(2,1)} %get-tuple-element.32.refs_1_.refs_3_.refs_2_, bf16[2048,1024]{1,0:T(8,128)(2,1)} %get-tuple-element.29.refs_3_.refs_2_.refs_1_, ...), custom_call_target="tpu_custom_call" | custom-call | flops 2000000000 | bytes 9482240 | tf_op jit(solution)/shard_map/pallas_call | solution.py:165
  22.4 0.1 collective-permute-start.1
  22.5 2.8 %shard_map.116.cot_ref = f32[512,256]{1,0:T(8,128)S(1)} custom-call(f32[8,136,128]{2,1,0:T(8,128)S(1)} %all-to-all-done.refs_0_.cot_ref, bf16[2048,1024]{1,0:T(8,128)(2,1)} %get-tuple-element.29.refs_3_.refs_2_.refs_1_, bf16[1024,1024]{1,0:T(8,128)(2,1)S(1)} %get-tuple-element.35.refs_2_), custom_call_target="tpu_custom_call" | custom-call | flops 2000000000 | bytes 6848512 | tf_op jit(solution)/shard_map/pallas_call | solution.py:165
  25.3 0.0 collective-permute-done.feat_got_ref
  25.3 0.0 collective-permute-done.1.cot_got_ref
  25.3 0.1 shard_map.117
  25.4 24.1 %all_to_all.20.parts_ref = f32[8,64,512]{2,1,0:T(8,128)S(1)} all-to-all(f32[8,64,512]{2,1,0:T(8,128)S(1)} %shard_map.117), channel_id=1, replica_groups={{0,16,32,48,64,80,96,112},{8,24,40,56,72,88,104,120},{1,17,33,49,65,81,..., dimensions={0} | all-to-all | bytes 2097152 | tf_op jit(solution)/shard_map/all_to_all | solution.py:613
  49.5 0.1 shard_map.118
  49.6 20.1 %all_to_all.21 = f32[8,64,512]{2,1,0:T(8,128)S(1)} all-to-all(f32[8,64,512]{2,1,0:T(8,128)S(1)} %shard_map.118), channel_id=1, replica_groups={{0,16,32,48,64,80,96,112},{8,24,40,56,72,88,104,120},{1,17,33,49,65,81,..., dimensions={0} | all-to-all | bytes 2097152 | tf_op jit(solution)/shard_map/all_to_all | solution.py:613
  69.7 0.0 collective-permute-start.2
  69.7 2.4 %collective-permute-start.3 = (f32[272,256]{1,0:T(8,128)S(1)}, f32[272,256]{1,0:T(8,128)S(1)}, u32[]{:S(2)}, u32[]{:S(2)}) collective-permute-start(f32[272,256]{1,0:T(8,128)S(1)} %get-tuple-element.39), channel_id=1, source_target_pairs={{0,8},{15,7},{1,9},{14,6},{8,16},{23,15},{9,17},{22,14},{16,24},{3... | collective-permute-start | bytes 835592 | tf_op jit(solution)/shard_map/ppermute | solution.py:639
  72.1 3.7 %shard_map.119 = (f32[256,1024]{1,0:T(8,128)S(1)}, bf16[1024,1024]{1,0:T(8,128)(2,1)S(1)}, f32[128,1024]{1,0:T(8,128)S(1)}) custom-call(f32[512,512]{1,0:T(8,128)S(1)} %bitcast.2, f32[128,1024]{1,0:T(8,128)} %refs_1_.1, bf16[2048,1024]{1,0:T(8,128)(2,1)} %get-tuple-element.29.refs_3_.refs_2_.refs_1_, bf16[2048,1024]{1,0:T(8,128)(2,1)} %get-tuple-element.32.refs_1_.refs_3_.refs_2_), custom_call_target="tpu_custom_call" | custom-call | flops 4000000000 | bytes 9961472 | tf_op jit(solution)/shard_map/pallas_call | solution.py:165
  75.8 0.0 collective-permute-done.2.refs_0_.oth_ref
  75.8 0.0 copy-start
  75.8 3.9 %shard_map.120 = f32[8,256,128]{2,1,0:T(8,128)} custom-call(f32[512,512]{1,0:T(8,128)S(1)} %collective-permute-done.2.refs_0_.oth_ref, f32[128,1024]{1,0:T(8,128)S(1)} %get-tuple-element.36.refs_1_, bf16[2048,1024]{1,0:T(8,128)(2,1)} %get-tuple-element.32.refs_1_.refs_3_.refs_2_, bf16[1024,1024]{1,0:T(8,128)(2,1)S(1)} %get-tuple-element.37.refs_3_, ...), custom_call_target="tpu_custom_call" | custom-call | flops 4000000000 | bytes 8912896 | tf_op jit(solution)/shard_map/pallas_call | solution.py:165
  79.7 0.0 copy-done
  79.7 0.0 copy-start.2
  79.7 0.0 copy-start.3
  79.7 0.0 copy-start.5
  79.7 1.4 %collective-permute-done.3.rim_ref = f32[272,256]{1,0:T(8,128)S(1)} collective-permute-done((f32[272,256]{1,0:T(8,128)S(1)}, f32[272,256]{1,0:T(8,128)S(1)}, u32[]{:S(2)}, u32[]{:S(2)}) %collective-permute-start.3) | collective-permute-done | bytes 278560 | tf_op jit(solution)/shard_map/ppermute | solution.py:639
  81.1 3.7 %all-to-all-start.3 = ((f32[8,256,128]{2,1,0:T(8,128)}), f32[8,256,128]{2,1,0:T(8,128)S(1)}, u32[]{:S(2)}, u32[]{:S(2)}) async-start(f32[8,256,128]{2,1,0:T(8,128)} %shard_map.120), calls=%async_computation.3 | async-start | bytes 2097152 | tf_op jit(solution)/shard_map/all_to_all | solution.py:656
  84.8 0.0 copy-start.1
  84.9 1.2 %copy-done.1 = f32[512,512]{1,0:T(8,128)S(1)} copy-done((f32[512,512]{1,0:T(8,128)S(1)}, f32[512,512]{1,0:T(8,128)}, u32[]{:S(2)}) %copy-start.1) | copy-done | bytes 1048600
  86.1 1.0 %shard_map.123 = f32[128,1024]{1,0:T(8,128)} custom-call(f32[512,512]{1,0:T(8,128)S(1)} %bitcast.3, f32[512,512]{1,0:T(8,128)S(1)} %copy-done.1), custom_call_target="tpu_custom_call" | custom-call | flops 100000000 | bytes 2097152 | tf_op jit(solution)/shard_map/pallas_call | solution.py:165
  87.1 0.0 copy-done.2
  87.1 0.0 copy-done.3
  87.1 0.0 copy-done.5
  87.1 0.0 copy-start.4
  87.1 0.9 copy-done.4
  88.0 3.3 %shard_map.121 = (f32[128,128]{1,0:T(8,128)S(1)}, f32[128,128]{1,0:T(8,128)S(1)}) custom-call(f32[272,256]{1,0:T(8,128)S(1)} %collective-permute-done.3.rim_ref, f32[128,1024]{1,0:T(8,128)S(1)} %copy-done.2, f32[3,1024]{1,0:T(4,128)S(1)} %copy-done.3, f32[8,136,128]{2,1,0:T(8,128)S(1)} %all-to-all-done.refs_0_.cot_ref, f32[4,128,128]{2,1,0:T(8,128)S(1)} %copy-done.4, ...), custom_call_target="tpu_custom_call" | custom-call | flops 2000000000 | bytes 1634320 | tf_op jit(solution)/shard_map/pallas_call | solution.py:165
  91.3 7.4 %all-to-all-done.3.parts_ref = f32[8,256,128]{2,1,0:T(8,128)S(1)} async-done(((f32[8,256,128]{2,1,0:T(8,128)}), f32[8,256,128]{2,1,0:T(8,128)S(1)}, u32[]{:S(2)}, u32[]{:S(2)}) %all-to-all-start.3) | async-done | bytes 1048608 | tf_op jit(solution)/shard_map/all_to_all | solution.py:656
  98.7 0.7 shard_map.122
Async XLA Ops:
  3.1 16.1 %all-to-all-start = ((f32[8,136,128]{2,1,0:T(8,128)}), f32[8,136,128]{2,1,0:T(8,128)S(1)}, u32[]{:S(2)}, u32[]{:S(2)}) async-start(f32[8,136,128]{2,1,0:T(8,128)} %get-tuple-element.27.refs_3_), calls=%async_computation | async-start | bytes 1114112 | tf_op jit(solution)/shard_map/all_to_all | solution.py:632
  18.5 6.7 %collective-permute-start = (f32[512,256]{1,0:T(8,128)S(1)}, f32[512,256]{1,0:T(8,128)S(1)}, u32[]{:S(2)}, u32[]{:S(2)}) collective-permute-start(f32[512,256]{1,0:T(8,128)S(1)} %get-tuple-element.30), channel_id=1, source_target_pairs={{0,8},{8,0},{16,24},{24,16},{32,40},{40,32},{48,56},{56,48},{64,72... | collective-permute-start | bytes 1572872 | tf_op jit(solution)/shard_map/ppermute | solution.py:636
  22.4 2.9 %collective-permute-start.1 = (f32[512,256]{1,0:T(8,128)S(1)}, f32[512,256]{1,0:T(8,128)S(1)}, u32[]{:S(2)}, u32[]{:S(2)}) collective-permute-start(f32[512,256]{1,0:T(8,128)S(1)} %get-tuple-element.33), channel_id=1, source_target_pairs={{0,8},{8,0},{16,24},{24,16},{32,40},{40,32},{48,56},{56,48},{64,72... | collective-permute-start | bytes 1572872 | tf_op jit(solution)/shard_map/ppermute | solution.py:640
  69.7 6.1 %collective-permute-start.2 = (f32[512,512]{1,0:T(8,128)S(1)}, f32[512,512]{1,0:T(8,128)S(1)}, u32[]{:S(2)}, u32[]{:S(2)}) collective-permute-start(f32[512,512]{1,0:T(8,128)S(1)} %bitcast.1), channel_id=1, source_target_pairs={{0,8},{8,0},{16,24},{24,16},{32,40},{40,32},{48,56},{56,48},{64,72... | collective-permute-start | bytes 3145736 | tf_op jit(solution)/shard_map/ppermute | solution.py:649
  69.7 11.5 %collective-permute-start.3 = (f32[272,256]{1,0:T(8,128)S(1)}, f32[272,256]{1,0:T(8,128)S(1)}, u32[]{:S(2)}, u32[]{:S(2)}) collective-permute-start(f32[272,256]{1,0:T(8,128)S(1)} %get-tuple-element.39), channel_id=1, source_target_pairs={{0,8},{15,7},{1,9},{14,6},{8,16},{23,15},{9,17},{22,14},{16,24},{3... | collective-permute-start | bytes 835592 | tf_op jit(solution)/shard_map/ppermute | solution.py:639
  75.8 3.9 %copy-start = (f32[512,512]{1,0:T(8,128)}, f32[512,512]{1,0:T(8,128)S(1)}, u32[]{:S(2)}) copy-start(f32[512,512]{1,0:T(8,128)S(1)} %collective-permute-done.2.refs_0_.oth_ref) | copy-start | bytes 3145732
  79.7 7.4 %copy-start.2 = (f32[128,1024]{1,0:T(8,128)S(1)}, f32[128,1024]{1,0:T(8,128)}, u32[]{:S(2)}) copy-start(f32[128,1024]{1,0:T(8,128)} %feat_ref.1) | copy-start | bytes 1572868
  79.7 7.4 %copy-start.3 = (f32[3,1024]{1,0:T(4,128)S(1)}, f32[3,1024]{1,0:T(4,128)}, u32[]{:S(2)}) copy-start(f32[3,1024]{1,0:T(4,128)} %pos_ref.1) | copy-start | bytes 36868
  79.7 7.4 %copy-start.5 = (f32[4]{0:T(128)S(1)}, f32[4]{0:T(128)}, u32[]{:S(2)}) copy-start(f32[4]{0:T(128)} %rate_ref.1) | copy-start | bytes 52
  81.1 17.6 %all-to-all-start.3 = ((f32[8,256,128]{2,1,0:T(8,128)}), f32[8,256,128]{2,1,0:T(8,128)S(1)}, u32[]{:S(2)}, u32[]{:S(2)}) async-start(f32[8,256,128]{2,1,0:T(8,128)} %shard_map.120), calls=%async_computation.3 | async-start | bytes 2097152 | tf_op jit(solution)/shard_map/all_to_all | solution.py:656
  84.8 1.2 %copy-start.1 = (f32[512,512]{1,0:T(8,128)S(1)}, f32[512,512]{1,0:T(8,128)}, u32[]{:S(2)}) copy-start(f32[512,512]{1,0:T(8,128)} %copy-done) | copy-start | bytes 3145732
  87.1 1.0 copy-start.4

commit v2 on v1

--- a/solution.py
+++ b/solution.py
@@ -53,6 +53,7 @@
 TILE = 256
 CHUNK = 4 * TILE
 TILES = HALF // TILE
+AHEAD = 2 * TILE
 
 
 def columns_of(rows):
@@ -93,11 +94,9 @@
         leave(tile * CHUNK + group * BLOCK)
 
 
-def sums_tile(tab_ref, rhs_ref, out_ref, tile, wide, copies=()):
+def sums_tile(tab_ref, rhs_ref, out_ref, tile, wide, high_ref):
     at = tile * CHUNK
-    for copy in copies:
-        copy.wait()
-    both = dot(tab_ref[at : at + 2 * TILE, :], rhs_ref[...], NT)
+    both = dot(high_ref[at : at + 2 * TILE, :], rhs_ref[...], NT)
     rest = dot(tab_ref[at + 2 * TILE : at + CHUNK, :], rhs_ref[0:wide, :], NT)
     total = both[:, :wide] + both[:, wide:] + rest
     for trig in range(2):
@@ -137,7 +136,7 @@
             high, low = pieces(feat_ref[...])
             rhs_ref[0:C, :] = high
             rhs_ref[C:, :] = low
-        sums_tile(tab_ref, rhs_ref, out_ref, tile, C)
+        sums_tile(tab_ref, rhs_ref, out_ref, tile, C, tab_ref)
     for copy in copies:
         copy.wait()
 
@@ -203,10 +202,11 @@
     )
 
 
-def fetched(tab_hbm, tab_ref, sems, tiles):
+def fetched(tab_hbm, tab_ref, sems, begun=False):
     copies = []
-    for tile in tiles:
-        rows = pl.ds(tile * CHUNK, CHUNK)
+    for tile in range(TILES):
+        skip = AHEAD if begun and tile == 0 else 0
+        rows = pl.ds(tile * CHUNK + skip, CHUNK - skip)
         copy = pltpu.make_async_copy(tab_hbm.at[rows], tab_ref.at[rows], sems.at[tile])
         copy.start()
         copies.append(copy)
@@ -214,15 +214,18 @@
 
 
 def ahead(next_hbm, next_ref, sem):
-    copy = pltpu.make_async_copy(next_hbm.at[pl.ds(0, CHUNK)], next_ref, sem)
+    copy = pltpu.make_async_copy(next_hbm.at[pl.ds(0, AHEAD)], next_ref, sem)
     copy.start()
     return copy
 
 
 def cot_kernel(first, cot_ref, tab_hbm, other_ref, *rest):
     if first:
-        feat_hbm, pos_hbm, out_ref, next_ref, rim_ref, rhs_ref, tab_ref, sems, pos_ref = rest
-        copies = fetched(tab_hbm, tab_ref, sems, range(TILES))
+        feat_hbm, pos_hbm, sums_ref, out_ref, next_ref, rim_ref = rest[:6]
+        rhs_ref, tab_ref, sems, pos_ref = rest[6:]
+        out_ref[:, 0 : 2 * C] = sums_ref[...]
+        out_ref = out_ref.at[:, 2 * C :]
+        copies = fetched(tab_hbm, tab_ref, sems)
         pad = REACH * BLOCK
         tail = lax.axis_index("mode") < MODE_DEV // 2
         block = jnp.where(tail, MODE_DEV - REACH, 0)
@@ -241,14 +244,12 @@
         rim_ref[C : C + 8, :] = jnp.zeros((8, pad), F32)
     else:
         out_ref, rhs_ref, tab_ref, sems = rest
-        copies = [None] + fetched(tab_hbm, tab_ref, sems, range(1, TILES))
+        copies = fetched(tab_hbm, tab_ref, sems, begun=True)
     cot_rows(cot_ref, rhs_ref, 0, C)
     for tile in range(TILES):
-        if copies[tile] is None:
-            sums_tile(other_ref, rhs_ref, out_ref, tile, C)
-        else:
-            copies[tile].wait()
-            sums_tile(tab_ref, rhs_ref, out_ref, tile, C)
+        copies[tile].wait()
+        high_ref = other_ref if tile == 0 and not first else tab_ref
+        sums_tile(tab_ref, rhs_ref, out_ref, tile, C, high_ref)
     if first:
         for copy in later:
             copy.wait()
@@ -259,14 +260,14 @@
     def body(*refs):
         cot_kernel(first, *refs)
 
-    outs = [((HALF, 2 * C), F32)]
+    outs = [((HALF, 4 * C if first else 2 * C), F32)]
     scratch = [
         VMEM((2 * C, ATOMS), BF16),
         VMEM((4 * HALF, ATOMS), BF16),
         pltpu.SemaphoreType.DMA((TILES + 3,)),
     ]
     if first:
-        outs += [((CHUNK, ATOMS), BF16), ((HALO_ROWS, REACH * BLOCK), F32)]
+        outs += [((AHEAD, ATOMS), BF16), ((HALO_ROWS, REACH * BLOCK), F32)]
         scratch.append(VMEM((3, ATOMS), F32))
     return call(
         body,
@@ -278,16 +279,21 @@
     )
 
 
-def merge_kernel(feat_ref, cot_ref, feat_got_ref, cot_got_ref, out_ref):
+def merge_kernel(feat_ref, cot_ref, got_ref, out_hbm, out_ref, sems):
+    copies = []
     for k in range(8):
         rows = slice(k * SHARE, (k + 1) * SHARE)
         for trig in range(2):
             for part in range(2):
                 lanes = slice((2 * trig + part) * C, (2 * trig + part + 1) * C)
                 here = slice(trig * C, (trig + 1) * C)
+                there = slice((2 * part + trig) * C, (2 * part + trig + 1) * C)
                 own = (feat_ref, cot_ref)[part]
-                got = (feat_got_ref, cot_got_ref)[part]
-                out_ref[k, :, lanes] = own[rows, here] + got[rows, here]
+                out_ref[k, :, lanes] = own[rows, here] + got_ref[rows, there]
+        copies.append(pltpu.make_async_copy(out_ref.at[k], out_hbm.at[k], sems.at[k]))
+        copies[-1].start()
+    for copy in copies:
+        copy.wait()
 
 
 def give_back_kernel(own, sums_ref, filt_hbm, tab_hbm, other_ref, *rest):
@@ -301,10 +307,10 @@
     if own:
         fetch = pltpu.make_async_copy(filt_hbm, filt_ref, sems.at[TILES])
         fetch.start()
-        copies = fetched(tab_hbm, tab_ref, sems, range(TILES))
+        copies = fetched(tab_hbm, tab_ref, sems)
         later = ahead(other_ref, next_ref, sems.at[TILES + 1])
     else:
-        copies = [None] + fetched(tab_hbm, tab_ref, sems, range(1, TILES))
+        copies = fetched(tab_hbm, tab_ref, sems, begun=True)
     if own:
         fetch.wait()
     scale = 1.0 / (ATOM_DEV * ATOMS)
@@ -321,17 +327,16 @@
     width = 2 * BLOCK
     stores = []
     for n in range(TILES):
-        if copies[n] is not None:
-            copies[n].wait()
-        table = other_ref if copies[n] is None else tab_ref
+        copies[n].wait()
+        high_ref = other_ref if n == 0 and not own else tab_ref
         depth = slice(n * 2 * TILE, (n + 1) * 2 * TILE)
         for k in range(ATOMS // width):
             lanes = slice(k * width, (k + 1) * width)
             top = n * CHUNK
-            both = dot(lhs_ref[:, depth], table[top : top + 2 * TILE, lanes], NN)
+            both = dot(lhs_ref[:, depth], high_ref[top : top + 2 * TILE, lanes], NN)
             more = dot(
                 lhs_ref[0 : 2 * C, depth],
-                table[top + 2 * TILE : top + CHUNK, lanes],
+                tab_ref[top + 2 * TILE : top + CHUNK, lanes],
                 NN,
             )
             part = both[: 2 * C] + both[2 * C :] + more
@@ -367,7 +372,7 @@
 
     args = [sums, filt, tab, other]
     if own:
-        outs = [((2 * C, ATOMS), F32), ((CHUNK, ATOMS), BF16), ((C, MODES), F32)]
+        outs = [((2 * C, ATOMS), F32), ((AHEAD, ATOMS), BF16), ((C, MODES), F32)]
     else:
         args.append(acc)
         outs = [((MODE_DEV, 2 * C, BLOCK), F32)]
@@ -633,15 +638,20 @@
 
     f_own, tab_own = tables_call(True, features, pos_near, wave_near, packed)
     f_oth, tab_oth = tables_call(False, features, pos_near, wave_near, tab_own)
-    f_got = lax.ppermute(f_oth, "atom", core_swap)
     cot, f_oth = lax.optimization_barrier((cot, f_oth))
-    c_oth, tab_next, rim = cot_call(True, cot, tab_oth, tab_own, features, positions)
+    oth, tab_next, rim = cot_call(
+        True, cot, tab_oth, tab_own, features, positions, f_oth
+    )
     rim = lax.ppermute(rim, ("atom", "mode"), rims)
-    c_got = lax.ppermute(c_oth, "atom", core_swap)
-    cot, c_oth = lax.optimization_barrier((cot, c_oth))
+    got = lax.ppermute(oth, "atom", core_swap)
+    cot, oth = lax.optimization_barrier((cot, oth))
     (c_own,) = cot_call(False, cot, tab_own, tab_next)
     (parts,) = call(
-        merge_kernel, (f_own, c_own, f_got, c_got), (((8, SHARE, 4 * C), F32),)
+        merge_kernel,
+        (f_own, c_own, got),
+        (((8, SHARE, 4 * C), F32),),
+        [VMEM((8, SHARE, 4 * C), F32), pltpu.SemaphoreType.DMA((8,))],
+        far_outs=(0,),
     )
     parts = exchange(parts)
     (share,) = call(share_kernel, (parts,), ((parts.shape, F32),))

time: 100 us -> 102 us (1.020)
  Pallas kernels: 29.5 us -> 31.1 us
  starting transfers between devices: 12.6 us -> 13.7 us
    pallas_call x12, Pallas kernels: 29.5 us -> 31.1 us  [call(): pl.pallas_call(body, out_shape=tuple((pltpu.HBM(shape, kind) if k in far_...]
    all_to_all x1, starting transfers between devices: 3.7 us -> 4.85 us  [per_device(): back = lax.all_to_all(back, 'mode', 0, 0, tiled=True)]
  transfers between devices with their start and end apart: 6 -> 5, of which waited for: 3 -> 3; matrix products, arithmetic and copies ran while one was open for 0% -> 0% of each run, Pallas kernels for 27% -> 24%
where the time goes in v2:
time: 102 us
  blocking collectives  44.4 us (44%)
  Pallas kernels  31.1 us (30%)
  starting transfers between devices  13.7 us (13%)
  waiting for transfers between devices  9.02 us (9%)
  local copies, waits for them, and re-layouts  2.19 us (2%)
  between operations  1.44 us (1%)
    all_to_all x2, blocking collectives, exchange(): return lax.all_to_all(x, 'atom', 0, 0, axis_index_groups=chips, tiled=True)  44.4 us
    pallas_call x12, Pallas kernels, call(): pl.pallas_call(body, out_shape=tuple((pltpu.HBM(shape, kind) if k in far_...  31.1 us
    all_to_all x1, waiting for transfers between devices, per_device(): back = lax.all_to_all(back, 'mode', 0, 0, tiled=True)  7.49 us
    all_to_all x1, starting transfers between devices, per_device(): cot = lax.all_to_all(packed, 'mode', 0, 0, tiled=True)  6.36 us
    all_to_all x1, starting transfers between devices, per_device(): back = lax.all_to_all(back, 'mode', 0, 0, tiled=True)  4.85 us
    ppermute x1, starting transfers between devices, per_device(): rim = lax.ppermute(rim, ('atom', 'mode'), rims)  2.4 us
    unnamed x12, local copies, waits for them, and re-layouts  2.19 us
  transfers between devices with their start and end apart: 5, of which 3 were waited for; matrix products, arithmetic and copies ran while one was open for 0% of the time, Pallas kernels for 24%

profile of v2, /device:TPU:0, one launch (start us, length us, event | category | flops | bytes accessed | tf_op | source)
XLA Modules:
  0.0 101.9 jit_solution(14415424903556150541)
XLA Ops:
  1.3 1.8 %shard_map.112 = (f32[8,136,128]{2,1,0:T(8,128)}, f32[3,1024]{1,0:T(4,128)S(1)}, s32[3,1024]{1,0:T(4,128)S(1)}) custom-call(s32[1,5]{1,0:T(1,128)} %ids_hbm.1, s32[1]{0:T(128)S(6)} %copy.12.live_ref, f32[128,128]{1,0:T(8,128)} %cot_hbm.1, f32[3,1024]{1,0:T(4,128)} %pos_ref.1, s32[3,1024]{1,0:T(4,128)} %wave_hbm.1), custom_call_target="tpu_custom_call" | custom-call | flops 100000000 | bytes 90136 | tf_op jit(solution)/shard_map/pallas_call | solution.py:164
  3.1 6.4 %all-to-all-start = ((f32[8,136,128]{2,1,0:T(8,128)}), f32[8,136,128]{2,1,0:T(8,128)S(1)}, u32[]{:S(2)}, u32[]{:S(2)}) async-start(f32[8,136,128]{2,1,0:T(8,128)} %get-tuple-element.28.refs_3_), calls=%async_computation | async-start | bytes 1114112 | tf_op jit(solution)/shard_map/all_to_all | solution.py:637
  9.5 4.5 %shard_map.113 = (f32[512,256]{1,0:T(8,128)S(1)}, bf16[2048,1024]{1,0:T(8,128)(2,1)}) custom-call(f32[128,1024]{1,0:T(8,128)} %feat_ref.1, f32[3,1024]{1,0:T(4,128)S(1)} %get-tuple-element.26.refs_1_, s32[3,1024]{1,0:T(4,128)S(1)} %get-tuple-element.27.refs_2_, f32[8,136,128]{2,1,0:T(8,128)} %get-tuple-element.28.refs_3_), custom_call_target="tpu_custom_call" | custom-call | flops 4000000000 | bytes 1105920 | tf_op jit(solution)/shard_map/pallas_call | solution.py:164
  14.0 4.5 %shard_map.114 = (f32[512,256]{1,0:T(8,128)S(1)}, bf16[2048,1024]{1,0:T(8,128)(2,1)}) custom-call(f32[128,1024]{1,0:T(8,128)} %feat_ref.1, f32[3,1024]{1,0:T(4,128)S(1)} %get-tuple-element.26.refs_1_, s32[3,1024]{1,0:T(4,128)S(1)} %get-tuple-element.27.refs_2_, bf16[2048,1024]{1,0:T(8,128)(2,1)} %get-tuple-element.30.refs_3_.refs_2_.refs_1_), custom_call_target="tpu_custom_call" | custom-call | flops 4000000000 | bytes 4743168 | tf_op jit(solution)/shard_map/pallas_call | solution.py:164
  18.5 0.7 all-to-all-done.refs_0_.cot_ref
  19.2 3.1 %shard_map.115 = (f32[512,512]{1,0:T(8,128)S(1)}, bf16[512,1024]{1,0:T(8,128)(2,1)S(1)}, f32[272,256]{1,0:T(8,128)S(1)}) custom-call(f32[8,136,128]{2,1,0:T(8,128)S(1)} %all-to-all-done.refs_0_.cot_ref, bf16[2048,1024]{1,0:T(8,128)(2,1)} %get-tuple-element.33.refs_1_.refs_3_.refs_2_, bf16[2048,1024]{1,0:T(8,128)(2,1)} %get-tuple-element.30.refs_3_.refs_2_.refs_1_, ...), custom_call_target="tpu_custom_call" | custom-call | flops 2000000000 | bytes 10006528 | tf_op jit(solution)/shard_map/pallas_call | solution.py:164
  22.4 0.1 collective-permute-start
  22.5 2.8 %shard_map.116.cot_ref = f32[512,256]{1,0:T(8,128)S(1)} custom-call(f32[8,136,128]{2,1,0:T(8,128)S(1)} %all-to-all-done.refs_0_.cot_ref, bf16[2048,1024]{1,0:T(8,128)(2,1)} %get-tuple-element.30.refs_3_.refs_2_.refs_1_, bf16[512,1024]{1,0:T(8,128)(2,1)S(1)} %get-tuple-element.37.refs_2_), custom_call_target="tpu_custom_call" | custom-call | flops 2000000000 | bytes 5799936 | tf_op jit(solution)/shard_map/pallas_call | solution.py:164
  25.2 0.0 collective-permute-done.got_ref
  25.2 1.1 %shard_map.117 = f32[8,64,512]{2,1,0:T(8,128)} custom-call(f32[512,256]{1,0:T(8,128)S(1)} %get-tuple-element.29.feat_ref, f32[512,256]{1,0:T(8,128)S(1)} %shard_map.116.cot_ref, f32[512,512]{1,0:T(8,128)S(1)} %collective-permute-done.got_ref), custom_call_target="tpu_custom_call" | custom-call | flops 100000000 | bytes 2097152 | tf_op jit(solution)/shard_map/pallas_call | solution.py:164
  26.4 24.3 %all_to_all.20.parts_ref = f32[8,64,512]{2,1,0:T(8,128)S(1)} all-to-all(f32[8,64,512]{2,1,0:T(8,128)} %shard_map.117), channel_id=1, replica_groups={{0,16,32,48,64,80,96,112},{8,24,40,56,72,88,104,120},{1,17,33,49,65,81,..., dimensions={0} | all-to-all | bytes 2097152 | tf_op jit(solution)/shard_map/all_to_all | solution.py:618
  50.7 0.1 shard_map.118
  50.8 20.1 %all_to_all.21 = f32[8,64,512]{2,1,0:T(8,128)S(1)} all-to-all(f32[8,64,512]{2,1,0:T(8,128)S(1)} %shard_map.118), channel_id=1, replica_groups={{0,16,32,48,64,80,96,112},{8,24,40,56,72,88,104,120},{1,17,33,49,65,81,..., dimensions={0} | all-to-all | bytes 2097152 | tf_op jit(solution)/shard_map/all_to_all | solution.py:618
  70.9 0.0 collective-permute-start.1
  70.9 2.4 %collective-permute-start.2 = (f32[272,256]{1,0:T(8,128)S(1)}, f32[272,256]{1,0:T(8,128)S(1)}, u32[]{:S(2)}, u32[]{:S(2)}) collective-permute-start(f32[272,256]{1,0:T(8,128)S(1)} %get-tuple-element.41), channel_id=1, source_target_pairs={{0,8},{15,7},{1,9},{14,6},{8,16},{23,15},{9,17},{22,14},{16,24},{3... | collective-permute-start | bytes 835592 | tf_op jit(solution)/shard_map/ppermute | solution.py:645
  73.3 3.7 %shard_map.119 = (f32[256,1024]{1,0:T(8,128)S(1)}, bf16[512,1024]{1,0:T(8,128)(2,1)S(1)}, f32[128,1024]{1,0:T(8,128)S(1)}) custom-call(f32[512,512]{1,0:T(8,128)S(1)} %bitcast.2, f32[128,1024]{1,0:T(8,128)} %refs_1_.1, bf16[2048,1024]{1,0:T(8,128)(2,1)} %get-tuple-element.30.refs_3_.refs_2_.refs_1_, bf16[2048,1024]{1,0:T(8,128)(2,1)} %get-tuple-element.33.refs_1_.refs_3_.refs_2_), custom_call_target="tpu_custom_call" | custom-call | flops 4000000000 | bytes 9961472 | tf_op jit(solution)/shard_map/pallas_call | solution.py:164
  77.0 0.0 collective-permute-done.1.refs_0_.oth_ref
  77.0 0.0 copy-start
  77.0 4.5 %shard_map.120 = f32[8,256,128]{2,1,0:T(8,128)} custom-call(f32[512,512]{1,0:T(8,128)S(1)} %collective-permute-done.1.refs_0_.oth_ref, f32[128,1024]{1,0:T(8,128)S(1)} %get-tuple-element.38.refs_1_, bf16[2048,1024]{1,0:T(8,128)(2,1)} %get-tuple-element.33.refs_1_.refs_3_.refs_2_, bf16[512,1024]{1,0:T(8,128)(2,1)S(1)} %get-tuple-element.39.refs_3_, ...), custom_call_target="tpu_custom_call" | custom-call | flops 4000000000 | bytes 7864320 | tf_op jit(solution)/shard_map/pallas_call | solution.py:164
  81.5 0.0 copy-done
  81.5 0.0 copy-start.2
  81.5 0.0 copy-start.3
  81.5 0.0 copy-start.5
  81.5 0.8 collective-permute-done.2.rim_ref
  82.4 4.8 %all-to-all-start.3 = ((f32[8,256,128]{2,1,0:T(8,128)}), f32[8,256,128]{2,1,0:T(8,128)S(1)}, u32[]{:S(2)}, u32[]{:S(2)}) async-start(f32[8,256,128]{2,1,0:T(8,128)} %shard_map.120), calls=%async_computation.3 | async-start | bytes 2097152 | tf_op jit(solution)/shard_map/all_to_all | solution.py:666
  87.2 0.0 copy-start.1
  87.2 1.2 %copy-done.1 = f32[512,512]{1,0:T(8,128)S(1)} copy-done((f32[512,512]{1,0:T(8,128)S(1)}, f32[512,512]{1,0:T(8,128)}, u32[]{:S(2)}) %copy-start.1) | copy-done | bytes 1048600
  88.4 1.0 shard_map.123
  89.4 0.0 copy-done.2
  89.4 0.0 copy-done.3
  89.4 0.0 copy-done.5
  89.4 0.0 copy-start.4
  89.4 0.9 copy-done.4
  90.4 3.3 %shard_map.121 = (f32[128,128]{1,0:T(8,128)S(1)}, f32[128,128]{1,0:T(8,128)S(1)}) custom-call(f32[272,256]{1,0:T(8,128)S(1)} %collective-permute-done.2.rim_ref, f32[128,1024]{1,0:T(8,128)S(1)} %copy-done.2, f32[3,1024]{1,0:T(4,128)S(1)} %copy-done.3, f32[8,136,128]{2,1,0:T(8,128)S(1)} %all-to-all-done.refs_0_.cot_ref, f32[4,128,128]{2,1,0:T(8,128)S(1)} %copy-done.4, ...), custom_call_target="tpu_custom_call" | custom-call | flops 2000000000 | bytes 1634320 | tf_op jit(solution)/shard_map/pallas_call | solution.py:164
  93.7 7.5 %all-to-all-done.3.parts_ref = f32[8,256,128]{2,1,0:T(8,128)S(1)} async-done(((f32[8,256,128]{2,1,0:T(8,128)}), f32[8,256,128]{2,1,0:T(8,128)S(1)}, u32[]{:S(2)}, u32[]{:S(2)}) %all-to-all-start.3) | async-done | bytes 1048608 | tf_op jit(solution)/shard_map/all_to_all | solution.py:666
  101.2 0.7 shard_map.122
Async XLA Ops:
  3.1 16.1 %all-to-all-start = ((f32[8,136,128]{2,1,0:T(8,128)}), f32[8,136,128]{2,1,0:T(8,128)S(1)}, u32[]{:S(2)}, u32[]{:S(2)}) async-start(f32[8,136,128]{2,1,0:T(8,128)} %get-tuple-element.28.refs_3_), calls=%async_computation | async-start | bytes 1114112 | tf_op jit(solution)/shard_map/all_to_all | solution.py:637
  22.4 2.9 %collective-permute-start = (f32[512,512]{1,0:T(8,128)S(1)}, f32[512,512]{1,0:T(8,128)S(1)}, u32[]{:S(2)}, u32[]{:S(2)}) collective-permute-start(f32[512,512]{1,0:T(8,128)S(1)} %get-tuple-element.35), channel_id=1, source_target_pairs={{0,8},{8,0},{16,24},{24,16},{32,40},{40,32},{48,56},{56,48},{64,72... | collective-permute-start | bytes 3145736 | tf_op jit(solution)/shard_map/ppermute | solution.py:646
  70.9 6.1 %collective-permute-start.1 = (f32[512,512]{1,0:T(8,128)S(1)}, f32[512,512]{1,0:T(8,128)S(1)}, u32[]{:S(2)}, u32[]{:S(2)}) collective-permute-start(f32[512,512]{1,0:T(8,128)S(1)} %bitcast.1), channel_id=1, source_target_pairs={{0,8},{8,0},{16,24},{24,16},{32,40},{40,32},{48,56},{56,48},{64,72... | collective-permute-start | bytes 3145736 | tf_op jit(solution)/shard_map/ppermute | solution.py:659
  70.9 11.5 %collective-permute-start.2 = (f32[272,256]{1,0:T(8,128)S(1)}, f32[272,256]{1,0:T(8,128)S(1)}, u32[]{:S(2)}, u32[]{:S(2)}) collective-permute-start(f32[272,256]{1,0:T(8,128)S(1)} %get-tuple-element.41), channel_id=1, source_target_pairs={{0,8},{15,7},{1,9},{14,6},{8,16},{23,15},{9,17},{22,14},{16,24},{3... | collective-permute-start | bytes 835592 | tf_op jit(solution)/shard_map/ppermute | solution.py:645
  77.0 4.5 %copy-start = (f32[512,512]{1,0:T(8,128)}, f32[512,512]{1,0:T(8,128)S(1)}, u32[]{:S(2)}) copy-start(f32[512,512]{1,0:T(8,128)S(1)} %collective-permute-done.1.refs_0_.oth_ref) | copy-start | bytes 3145732
  81.5 7.9 %copy-start.2 = (f32[128,1024]{1,0:T(8,128)S(1)}, f32[128,1024]{1,0:T(8,128)}, u32[]{:S(2)}) copy-start(f32[128,1024]{1,0:T(8,128)} %feat_ref.1) | copy-start | bytes 1572868
  81.5 7.9 %copy-start.3 = (f32[3,1024]{1,0:T(4,128)S(1)}, f32[3,1024]{1,0:T(4,128)}, u32[]{:S(2)}) copy-start(f32[3,1024]{1,0:T(4,128)} %pos_ref.1) | copy-start | bytes 36868
  81.5 7.9 %copy-start.5 = (f32[4]{0:T(128)S(1)}, f32[4]{0:T(128)}, u32[]{:S(2)}) copy-start(f32[4]{0:T(128)} %rate_ref.1) | copy-start | bytes 52
  82.4 18.8 %all-to-all-start.3 = ((f32[8,256,128]{2,1,0:T(8,128)}), f32[8,256,128]{2,1,0:T(8,128)S(1)}, u32[]{:S(2)}, u32[]{:S(2)}) async-start(f32[8,256,128]{2,1,0:T(8,128)} %shard_map.120), calls=%async_computation.3 | async-start | bytes 2097152 | tf_op jit(solution)/shard_map/all_to_all | solution.py:666
  87.2 1.2 %copy-start.1 = (f32[512,512]{1,0:T(8,128)S(1)}, f32[512,512]{1,0:T(8,128)}, u32[]{:S(2)}) copy-start(f32[512,512]{1,0:T(8,128)} %copy-done) | copy-start | bytes 3145732
  89.4 1.0 copy-start.4

commit v3 on v1

--- a/solution.py
+++ b/solution.py
@@ -221,7 +221,10 @@
 
 def cot_kernel(first, cot_ref, tab_hbm, other_ref, *rest):
     if first:
-        feat_hbm, pos_hbm, out_ref, next_ref, rim_ref, rhs_ref, tab_ref, sems, pos_ref = rest
+        feat_hbm, pos_hbm, sums_ref, out_ref, next_ref, rim_ref = rest[:6]
+        rhs_ref, tab_ref, sems, pos_ref = rest[6:]
+        out_ref[:, 0 : 2 * C] = sums_ref[...]
+        out_ref = out_ref.at[:, 2 * C :]
         copies = fetched(tab_hbm, tab_ref, sems, range(TILES))
         pad = REACH * BLOCK
         tail = lax.axis_index("mode") < MODE_DEV // 2
@@ -259,7 +262,7 @@
     def body(*refs):
         cot_kernel(first, *refs)
 
-    outs = [((HALF, 2 * C), F32)]
+    outs = [((HALF, 4 * C if first else 2 * C), F32)]
     scratch = [
         VMEM((2 * C, ATOMS), BF16),
         VMEM((4 * HALF, ATOMS), BF16),
@@ -278,16 +281,21 @@
     )
 
 
-def merge_kernel(feat_ref, cot_ref, feat_got_ref, cot_got_ref, out_ref):
+def merge_kernel(feat_ref, cot_ref, got_ref, out_hbm, out_ref, sems):
+    copies = []
     for k in range(8):
         rows = slice(k * SHARE, (k + 1) * SHARE)
         for trig in range(2):
             for part in range(2):
                 lanes = slice((2 * trig + part) * C, (2 * trig + part + 1) * C)
                 here = slice(trig * C, (trig + 1) * C)
+                there = slice((2 * part + trig) * C, (2 * part + trig + 1) * C)
                 own = (feat_ref, cot_ref)[part]
-                got = (feat_got_ref, cot_got_ref)[part]
-                out_ref[k, :, lanes] = own[rows, here] + got[rows, here]
+                out_ref[k, :, lanes] = own[rows, here] + got_ref[rows, there]
+        copies.append(pltpu.make_async_copy(out_ref.at[k], out_hbm.at[k], sems.at[k]))
+        copies[-1].start()
+    for copy in copies:
+        copy.wait()
 
 
 def give_back_kernel(own, sums_ref, filt_hbm, tab_hbm, other_ref, *rest):
@@ -633,15 +641,20 @@
 
     f_own, tab_own = tables_call(True, features, pos_near, wave_near, packed)
     f_oth, tab_oth = tables_call(False, features, pos_near, wave_near, tab_own)
-    f_got = lax.ppermute(f_oth, "atom", core_swap)
     cot, f_oth = lax.optimization_barrier((cot, f_oth))
-    c_oth, tab_next, rim = cot_call(True, cot, tab_oth, tab_own, features, positions)
+    oth, tab_next, rim = cot_call(
+        True, cot, tab_oth, tab_own, features, positions, f_oth
+    )
     rim = lax.ppermute(rim, ("atom", "mode"), rims)
-    c_got = lax.ppermute(c_oth, "atom", core_swap)
-    cot, c_oth = lax.optimization_barrier((cot, c_oth))
+    got = lax.ppermute(oth, "atom", core_swap)
+    cot, oth = lax.optimization_barrier((cot, oth))
     (c_own,) = cot_call(False, cot, tab_own, tab_next)
     (parts,) = call(
-        merge_kernel, (f_own, c_own, f_got, c_got), (((8, SHARE, 4 * C), F32),)
+        merge_kernel,
+        (f_own, c_own, got),
+        (((8, SHARE, 4 * C), F32),),
+        [VMEM((8, SHARE, 4 * C), F32), pltpu.SemaphoreType.DMA((8,))],
+        far_outs=(0,),
     )
     parts = exchange(parts)
     (share,) = call(share_kernel, (parts,), ((parts.shape, F32),))

time: 100 us -> 102 us (1.020)
  transfers between devices with their start and end apart: 6 -> 5, of which waited for: 3 -> 3; matrix products, arithmetic and copies ran while one was open for 0% -> 0% of each run, Pallas kernels for 27% -> 23%
where the time goes in v3:
time: 102 us; the launch traced here: 101 us
  blocking collectives  44.6 us (44%)
  Pallas kernels  30.5 us (30%)
  starting transfers between devices  13.1 us (13%)
  waiting for transfers between devices  9.65 us (9%)
  local copies, waits for them, and re-layouts  2.19 us (2%)
  between operations  1.44 us (1%)
    all_to_all x2, blocking collectives, exchange(): return lax.all_to_all(x, 'atom', 0, 0, axis_index_groups=chips, tiled=True)  44.6 us
    pallas_call x12, Pallas kernels, call(): pl.pallas_call(body, out_shape=tuple((pltpu.HBM(shape, kind) if k in far_...  30.5 us
    all_to_all x1, waiting for transfers between devices, per_device(): back = lax.all_to_all(back, 'mode', 0, 0, tiled=True)  7.5 us
    all_to_all x1, starting transfers between devices, per_device(): cot = lax.all_to_all(packed, 'mode', 0, 0, tiled=True)  6.36 us
    all_to_all x1, starting transfers between devices, per_device(): back = lax.all_to_all(back, 'mode', 0, 0, tiled=True)  4.24 us
    ppermute x1, starting transfers between devices, per_device(): rim = lax.ppermute(rim, ('atom', 'mode'), rims)  2.4 us
    unnamed x12, local copies, waits for them, and re-layouts  2.19 us
  transfers between devices with their start and end apart: 5, of which 3 were waited for; matrix products, arithmetic and copies ran while one was open for 0% of the time, Pallas kernels for 23%

profile of v3, /device:TPU:0, one launch (start us, length us, event | category | flops | bytes accessed | tf_op | source)
XLA Modules:
  0.0 101.4 jit_solution(2434315694746241288)
XLA Ops:
  1.3 1.8 %shard_map.112 = (f32[8,136,128]{2,1,0:T(8,128)}, f32[3,1024]{1,0:T(4,128)S(1)}, s32[3,1024]{1,0:T(4,128)S(1)}) custom-call(s32[1,5]{1,0:T(1,128)} %ids_hbm.1, s32[1]{0:T(128)S(6)} %copy.12.live_ref, f32[128,128]{1,0:T(8,128)} %cot_hbm.1, f32[3,1024]{1,0:T(4,128)} %pos_ref.1, s32[3,1024]{1,0:T(4,128)} %wave_hbm.1), custom_call_target="tpu_custom_call" | custom-call | flops 100000000 | bytes 90136 | tf_op jit(solution)/shard_map/pallas_call | solution.py:165
  3.1 6.4 %all-to-all-start = ((f32[8,136,128]{2,1,0:T(8,128)}), f32[8,136,128]{2,1,0:T(8,128)S(1)}, u32[]{:S(2)}, u32[]{:S(2)}) async-start(f32[8,136,128]{2,1,0:T(8,128)} %get-tuple-element.28.refs_3_), calls=%async_computation | async-start | bytes 1114112 | tf_op jit(solution)/shard_map/all_to_all | solution.py:640
  9.5 4.5 %shard_map.113 = (f32[512,256]{1,0:T(8,128)S(1)}, bf16[2048,1024]{1,0:T(8,128)(2,1)}) custom-call(f32[128,1024]{1,0:T(8,128)} %feat_ref.1, f32[3,1024]{1,0:T(4,128)S(1)} %get-tuple-element.26.refs_1_, s32[3,1024]{1,0:T(4,128)S(1)} %get-tuple-element.27.refs_2_, f32[8,136,128]{2,1,0:T(8,128)} %get-tuple-element.28.refs_3_), custom_call_target="tpu_custom_call" | custom-call | flops 4000000000 | bytes 1105920 | tf_op jit(solution)/shard_map/pallas_call | solution.py:165
  14.0 4.5 %shard_map.114 = (f32[512,256]{1,0:T(8,128)S(1)}, bf16[2048,1024]{1,0:T(8,128)(2,1)}) custom-call(f32[128,1024]{1,0:T(8,128)} %feat_ref.1, f32[3,1024]{1,0:T(4,128)S(1)} %get-tuple-element.26.refs_1_, s32[3,1024]{1,0:T(4,128)S(1)} %get-tuple-element.27.refs_2_, bf16[2048,1024]{1,0:T(8,128)(2,1)} %get-tuple-element.30.refs_3_.refs_2_.refs_1_), custom_call_target="tpu_custom_call" | custom-call | flops 4000000000 | bytes 4743168 | tf_op jit(solution)/shard_map/pallas_call | solution.py:165
  18.5 0.7 all-to-all-done.refs_0_.cot_ref
  19.2 3.1 %shard_map.115 = (f32[512,512]{1,0:T(8,128)S(1)}, bf16[1024,1024]{1,0:T(8,128)(2,1)S(1)}, f32[272,256]{1,0:T(8,128)S(1)}) custom-call(f32[8,136,128]{2,1,0:T(8,128)S(1)} %all-to-all-done.refs_0_.cot_ref, bf16[2048,1024]{1,0:T(8,128)(2,1)} %get-tuple-element.33.refs_1_.refs_3_.refs_2_, bf16[2048,1024]{1,0:T(8,128)(2,1)} %get-tuple-element.30.refs_3_.refs_2_.refs_1_, ...), custom_call_target="tpu_custom_call" | custom-call | flops 2000000000 | bytes 10006528 | tf_op jit(solution)/shard_map/pallas_call | solution.py:165
  22.4 0.1 collective-permute-start
  22.5 2.8 %shard_map.116.cot_ref = f32[512,256]{1,0:T(8,128)S(1)} custom-call(f32[8,136,128]{2,1,0:T(8,128)S(1)} %all-to-all-done.refs_0_.cot_ref, bf16[2048,1024]{1,0:T(8,128)(2,1)} %get-tuple-element.30.refs_3_.refs_2_.refs_1_, bf16[1024,1024]{1,0:T(8,128)(2,1)S(1)} %get-tuple-element.37.refs_2_), custom_call_target="tpu_custom_call" | custom-call | flops 2000000000 | bytes 6848512 | tf_op jit(solution)/shard_map/pallas_call | solution.py:165
  25.2 0.0 collective-permute-done.got_ref
  25.3 1.1 %shard_map.117 = f32[8,64,512]{2,1,0:T(8,128)} custom-call(f32[512,256]{1,0:T(8,128)S(1)} %get-tuple-element.29.feat_ref, f32[512,256]{1,0:T(8,128)S(1)} %shard_map.116.cot_ref, f32[512,512]{1,0:T(8,128)S(1)} %collective-permute-done.got_ref), custom_call_target="tpu_custom_call" | custom-call | flops 100000000 | bytes 2097152 | tf_op jit(solution)/shard_map/pallas_call | solution.py:165
  26.4 24.3 %all_to_all.20.parts_ref = f32[8,64,512]{2,1,0:T(8,128)S(1)} all-to-all(f32[8,64,512]{2,1,0:T(8,128)} %shard_map.117), channel_id=1, replica_groups={{0,16,32,48,64,80,96,112},{8,24,40,56,72,88,104,120},{1,17,33,49,65,81,..., dimensions={0} | all-to-all | bytes 2097152 | tf_op jit(solution)/shard_map/all_to_all | solution.py:621
  50.7 0.1 shard_map.118
  50.8 20.2 %all_to_all.21 = f32[8,64,512]{2,1,0:T(8,128)S(1)} all-to-all(f32[8,64,512]{2,1,0:T(8,128)S(1)} %shard_map.118), channel_id=1, replica_groups={{0,16,32,48,64,80,96,112},{8,24,40,56,72,88,104,120},{1,17,33,49,65,81,..., dimensions={0} | all-to-all | bytes 2097152 | tf_op jit(solution)/shard_map/all_to_all | solution.py:621
  71.1 0.0 collective-permute-start.1
  71.1 2.4 %collective-permute-start.2 = (f32[272,256]{1,0:T(8,128)S(1)}, f32[272,256]{1,0:T(8,128)S(1)}, u32[]{:S(2)}, u32[]{:S(2)}) collective-permute-start(f32[272,256]{1,0:T(8,128)S(1)} %get-tuple-element.41), channel_id=1, source_target_pairs={{0,8},{15,7},{1,9},{14,6},{8,16},{23,15},{9,17},{22,14},{16,24},{3... | collective-permute-start | bytes 835592 | tf_op jit(solution)/shard_map/ppermute | solution.py:648
  73.5 3.7 %shard_map.119 = (f32[256,1024]{1,0:T(8,128)S(1)}, bf16[1024,1024]{1,0:T(8,128)(2,1)S(1)}, f32[128,1024]{1,0:T(8,128)S(1)}) custom-call(f32[512,512]{1,0:T(8,128)S(1)} %bitcast.2, f32[128,1024]{1,0:T(8,128)} %refs_1_.1, bf16[2048,1024]{1,0:T(8,128)(2,1)} %get-tuple-element.30.refs_3_.refs_2_.refs_1_, bf16[2048,1024]{1,0:T(8,128)(2,1)} %get-tuple-element.33.refs_1_.refs_3_.refs_2_), custom_call_target="tpu_custom_call" | custom-call | flops 4000000000 | bytes 9961472 | tf_op jit(solution)/shard_map/pallas_call | solution.py:165
  77.2 0.0 collective-permute-done.1.refs_0_.oth_ref
  77.2 0.0 copy-start
  77.2 3.9 %shard_map.120 = f32[8,256,128]{2,1,0:T(8,128)} custom-call(f32[512,512]{1,0:T(8,128)S(1)} %collective-permute-done.1.refs_0_.oth_ref, f32[128,1024]{1,0:T(8,128)S(1)} %get-tuple-element.38.refs_1_, bf16[2048,1024]{1,0:T(8,128)(2,1)} %get-tuple-element.33.refs_1_.refs_3_.refs_2_, bf16[1024,1024]{1,0:T(8,128)(2,1)S(1)} %get-tuple-element.39.refs_3_, ...), custom_call_target="tpu_custom_call" | custom-call | flops 4000000000 | bytes 8912896 | tf_op jit(solution)/shard_map/pallas_call | solution.py:165
  81.1 0.0 copy-done
  81.1 0.0 copy-start.2
  81.1 0.0 copy-start.3
  81.1 0.0 copy-start.5
  81.1 1.4 %collective-permute-done.2.rim_ref = f32[272,256]{1,0:T(8,128)S(1)} collective-permute-done((f32[272,256]{1,0:T(8,128)S(1)}, f32[272,256]{1,0:T(8,128)S(1)}, u32[]{:S(2)}, u32[]{:S(2)}) %collective-permute-start.2) | collective-permute-done | bytes 278560 | tf_op jit(solution)/shard_map/ppermute | solution.py:648
  82.5 4.2 %all-to-all-start.3 = ((f32[8,256,128]{2,1,0:T(8,128)}), f32[8,256,128]{2,1,0:T(8,128)S(1)}, u32[]{:S(2)}, u32[]{:S(2)}) async-start(f32[8,256,128]{2,1,0:T(8,128)} %shard_map.120), calls=%async_computation.3 | async-start | bytes 2097152 | tf_op jit(solution)/shard_map/all_to_all | solution.py:669
  86.8 0.0 copy-start.1
  86.8 1.2 %copy-done.1 = f32[512,512]{1,0:T(8,128)S(1)} copy-done((f32[512,512]{1,0:T(8,128)S(1)}, f32[512,512]{1,0:T(8,128)}, u32[]{:S(2)}) %copy-start.1) | copy-done | bytes 1048600
  88.0 1.0 shard_map.123
  89.0 0.0 copy-done.2
  89.0 0.0 copy-done.3
  89.0 0.0 copy-done.5
  89.0 0.0 copy-start.4
  89.0 0.9 copy-done.4
  90.0 3.3 %shard_map.121 = (f32[128,128]{1,0:T(8,128)S(1)}, f32[128,128]{1,0:T(8,128)S(1)}) custom-call(f32[272,256]{1,0:T(8,128)S(1)} %collective-permute-done.2.rim_ref, f32[128,1024]{1,0:T(8,128)S(1)} %copy-done.2, f32[3,1024]{1,0:T(4,128)S(1)} %copy-done.3, f32[8,136,128]{2,1,0:T(8,128)S(1)} %all-to-all-done.refs_0_.cot_ref, f32[4,128,128]{2,1,0:T(8,128)S(1)} %copy-done.4, ...), custom_call_target="tpu_custom_call" | custom-call | flops 2000000000 | bytes 1634320 | tf_op jit(solution)/shard_map/pallas_call | solution.py:165
  93.2 7.5 %all-to-all-done.3.parts_ref = f32[8,256,128]{2,1,0:T(8,128)S(1)} async-done(((f32[8,256,128]{2,1,0:T(8,128)}), f32[8,256,128]{2,1,0:T(8,128)S(1)}, u32[]{:S(2)}, u32[]{:S(2)}) %all-to-all-start.3) | async-done | bytes 1048608 | tf_op jit(solution)/shard_map/all_to_all | solution.py:669
  100.7 0.7 shard_map.122
Async XLA Ops:
  3.1 16.1 %all-to-all-start = ((f32[8,136,128]{2,1,0:T(8,128)}), f32[8,136,128]{2,1,0:T(8,128)S(1)}, u32[]{:S(2)}, u32[]{:S(2)}) async-start(f32[8,136,128]{2,1,0:T(8,128)} %get-tuple-element.28.refs_3_), calls=%async_computation | async-start | bytes 1114112 | tf_op jit(solution)/shard_map/all_to_all | solution.py:640
  22.4 2.9 %collective-permute-start = (f32[512,512]{1,0:T(8,128)S(1)}, f32[512,512]{1,0:T(8,128)S(1)}, u32[]{:S(2)}, u32[]{:S(2)}) collective-permute-start(f32[512,512]{1,0:T(8,128)S(1)} %get-tuple-element.35), channel_id=1, source_target_pairs={{0,8},{8,0},{16,24},{24,16},{32,40},{40,32},{48,56},{56,48},{64,72... | collective-permute-start | bytes 3145736 | tf_op jit(solution)/shard_map/ppermute | solution.py:649
  71.1 6.1 %collective-permute-start.1 = (f32[512,512]{1,0:T(8,128)S(1)}, f32[512,512]{1,0:T(8,128)S(1)}, u32[]{:S(2)}, u32[]{:S(2)}) collective-permute-start(f32[512,512]{1,0:T(8,128)S(1)} %bitcast.1), channel_id=1, source_target_pairs={{0,8},{8,0},{16,24},{24,16},{32,40},{40,32},{48,56},{56,48},{64,72... | collective-permute-start | bytes 3145736 | tf_op jit(solution)/shard_map/ppermute | solution.py:662
  71.1 11.5 %collective-permute-start.2 = (f32[272,256]{1,0:T(8,128)S(1)}, f32[272,256]{1,0:T(8,128)S(1)}, u32[]{:S(2)}, u32[]{:S(2)}) collective-permute-start(f32[272,256]{1,0:T(8,128)S(1)} %get-tuple-element.41), channel_id=1, source_target_pairs={{0,8},{15,7},{1,9},{14,6},{8,16},{23,15},{9,17},{22,14},{16,24},{3... | collective-permute-start | bytes 835592 | tf_op jit(solution)/shard_map/ppermute | solution.py:648
  77.2 3.9 %copy-start = (f32[512,512]{1,0:T(8,128)}, f32[512,512]{1,0:T(8,128)S(1)}, u32[]{:S(2)}) copy-start(f32[512,512]{1,0:T(8,128)S(1)} %collective-permute-done.1.refs_0_.oth_ref) | copy-start | bytes 3145732
  81.1 7.9 %copy-start.2 = (f32[128,1024]{1,0:T(8,128)S(1)}, f32[128,1024]{1,0:T(8,128)}, u32[]{:S(2)}) copy-start(f32[128,1024]{1,0:T(8,128)} %feat_ref.1) | copy-start | bytes 1572868
  81.1 7.9 %copy-start.3 = (f32[3,1024]{1,0:T(4,128)S(1)}, f32[3,1024]{1,0:T(4,128)}, u32[]{:S(2)}) copy-start(f32[3,1024]{1,0:T(4,128)} %pos_ref.1) | copy-start | bytes 36868
  81.1 7.9 %copy-start.5 = (f32[4]{0:T(128)S(1)}, f32[4]{0:T(128)}, u32[]{:S(2)}) copy-start(f32[4]{0:T(128)} %rate_ref.1) | copy-start | bytes 52
  82.5 18.2 %all-to-all-start.3 = ((f32[8,256,128]{2,1,0:T(8,128)}), f32[8,256,128]{2,1,0:T(8,128)S(1)}, u32[]{:S(2)}, u32[]{:S(2)}) async-start(f32[8,256,128]{2,1,0:T(8,128)} %shard_map.120), calls=%async_computation.3 | async-start | bytes 2097152 | tf_op jit(solution)/shard_map/all_to_all | solution.py:669
  86.8 1.2 %copy-start.1 = (f32[512,512]{1,0:T(8,128)S(1)}, f32[512,512]{1,0:T(8,128)}, u32[]{:S(2)}) copy-start(f32[512,512]{1,0:T(8,128)} %copy-done) | copy-start | bytes 3145732
  89.0 1.0 copy-start.4

commit v4 on v3

--- a/solution.py
+++ b/solution.py
@@ -307,9 +307,17 @@
     core = lax.axis_index("atom") % 2
     at = pl.multiple_of(HALF * (core if own else 1 - core), HALF)
     if own:
-        fetch = pltpu.make_async_copy(filt_hbm, filt_ref, sems.at[TILES])
+        mine = pl.ds(at, HALF)
+        fetch = pltpu.make_async_copy(
+            filt_hbm.at[:, mine], filt_ref.at[:, mine], sems.at[TILES]
+        )
         fetch.start()
         copies = fetched(tab_hbm, tab_ref, sems, range(TILES))
+        theirs = pl.ds(pl.multiple_of(HALF - at, HALF), HALF)
+        rest_fetch = pltpu.make_async_copy(
+            filt_hbm.at[:, theirs], filt_ref.at[:, theirs], sems.at[TILES + 2]
+        )
+        rest_fetch.start()
         later = ahead(other_ref, next_ref, sems.at[TILES + 1])
     else:
         copies = [None] + fetched(tab_hbm, tab_ref, sems, range(1, TILES))
@@ -366,6 +374,7 @@
     for store in stores:
         store.wait()
     if own:
+        rest_fetch.wait()
         later.wait()
 
 

time: 102 us -> 102 us (level)
  no operation moved by 1% of the time
where the time goes in v4:
time: 102 us; the launch traced here: 101 us
  blocking collectives  44.6 us (44%)
  Pallas kernels  30.4 us (30%)
  starting transfers between devices  13 us (13%)
  waiting for transfers between devices  9.7 us (10%)
  local copies, waits for them, and re-layouts  2.19 us (2%)
  between operations  1.44 us (1%)
    all_to_all x2, blocking collectives, exchange(): return lax.all_to_all(x, 'atom', 0, 0, axis_index_groups=chips, tiled=True)  44.6 us
    pallas_call x12, Pallas kernels, call(): pl.pallas_call(body, out_shape=tuple((pltpu.HBM(shape, kind) if k in far_...  30.4 us
    all_to_all x1, waiting for transfers between devices, per_device(): back = lax.all_to_all(back, 'mode', 0, 0, tiled=True)  7.49 us
    all_to_all x1, starting transfers between devices, per_device(): cot = lax.all_to_all(packed, 'mode', 0, 0, tiled=True)  6.36 us
    all_to_all x1, starting transfers between devices, per_device(): back = lax.all_to_all(back, 'mode', 0, 0, tiled=True)  4.17 us
    ppermute x1, starting transfers between devices, per_device(): rim = lax.ppermute(rim, ('atom', 'mode'), rims)  2.4 us
    unnamed x12, local copies, waits for them, and re-layouts  2.19 us
  transfers between devices with their start and end apart: 5, of which 3 were waited for; matrix products, arithmetic and copies ran while one was open for 0% of the time, Pallas kernels for 23%

profile of v4, /device:TPU:0, one launch (start us, length us, event | category | flops | bytes accessed | tf_op | source)
XLA Modules:
  0.0 101.4 jit_solution(7714819829478717099)
XLA Ops:
  1.3 1.8 %shard_map.112 = (f32[8,136,128]{2,1,0:T(8,128)}, f32[3,1024]{1,0:T(4,128)S(1)}, s32[3,1024]{1,0:T(4,128)S(1)}) custom-call(s32[1,5]{1,0:T(1,128)} %ids_hbm.1, s32[1]{0:T(128)S(6)} %copy.12.live_ref, f32[128,128]{1,0:T(8,128)} %cot_hbm.1, f32[3,1024]{1,0:T(4,128)} %pos_ref.1, s32[3,1024]{1,0:T(4,128)} %wave_hbm.1), custom_call_target="tpu_custom_call" | custom-call | flops 100000000 | bytes 90136 | tf_op jit(solution)/shard_map/pallas_call | solution.py:165
  3.1 6.4 %all-to-all-start = ((f32[8,136,128]{2,1,0:T(8,128)}), f32[8,136,128]{2,1,0:T(8,128)S(1)}, u32[]{:S(2)}, u32[]{:S(2)}) async-start(f32[8,136,128]{2,1,0:T(8,128)} %get-tuple-element.28.refs_3_), calls=%async_computation | async-start | bytes 1114112 | tf_op jit(solution)/shard_map/all_to_all | solution.py:649
  9.5 4.5 %shard_map.113 = (f32[512,256]{1,0:T(8,128)S(1)}, bf16[2048,1024]{1,0:T(8,128)(2,1)}) custom-call(f32[128,1024]{1,0:T(8,128)} %feat_ref.1, f32[3,1024]{1,0:T(4,128)S(1)} %get-tuple-element.26.refs_1_, s32[3,1024]{1,0:T(4,128)S(1)} %get-tuple-element.27.refs_2_, f32[8,136,128]{2,1,0:T(8,128)} %get-tuple-element.28.refs_3_), custom_call_target="tpu_custom_call" | custom-call | flops 4000000000 | bytes 1105920 | tf_op jit(solution)/shard_map/pallas_call | solution.py:165
  14.0 4.5 %shard_map.114 = (f32[512,256]{1,0:T(8,128)S(1)}, bf16[2048,1024]{1,0:T(8,128)(2,1)}) custom-call(f32[128,1024]{1,0:T(8,128)} %feat_ref.1, f32[3,1024]{1,0:T(4,128)S(1)} %get-tuple-element.26.refs_1_, s32[3,1024]{1,0:T(4,128)S(1)} %get-tuple-element.27.refs_2_, bf16[2048,1024]{1,0:T(8,128)(2,1)} %get-tuple-element.30.refs_3_.refs_2_.refs_1_), custom_call_target="tpu_custom_call" | custom-call | flops 4000000000 | bytes 4743168 | tf_op jit(solution)/shard_map/pallas_call | solution.py:165
  18.5 0.7 all-to-all-done.refs_0_.cot_ref
  19.2 3.1 %shard_map.115 = (f32[512,512]{1,0:T(8,128)S(1)}, bf16[1024,1024]{1,0:T(8,128)(2,1)S(1)}, f32[272,256]{1,0:T(8,128)S(1)}) custom-call(f32[8,136,128]{2,1,0:T(8,128)S(1)} %all-to-all-done.refs_0_.cot_ref, bf16[2048,1024]{1,0:T(8,128)(2,1)} %get-tuple-element.33.refs_1_.refs_3_.refs_2_, bf16[2048,1024]{1,0:T(8,128)(2,1)} %get-tuple-element.30.refs_3_.refs_2_.refs_1_, ...), custom_call_target="tpu_custom_call" | custom-call | flops 2000000000 | bytes 10006528 | tf_op jit(solution)/shard_map/pallas_call | solution.py:165
  22.4 0.1 collective-permute-start
  22.5 2.8 %shard_map.116.cot_ref = f32[512,256]{1,0:T(8,128)S(1)} custom-call(f32[8,136,128]{2,1,0:T(8,128)S(1)} %all-to-all-done.refs_0_.cot_ref, bf16[2048,1024]{1,0:T(8,128)(2,1)} %get-tuple-element.30.refs_3_.refs_2_.refs_1_, bf16[1024,1024]{1,0:T(8,128)(2,1)S(1)} %get-tuple-element.37.refs_2_), custom_call_target="tpu_custom_call" | custom-call | flops 2000000000 | bytes 6848512 | tf_op jit(solution)/shard_map/pallas_call | solution.py:165
  25.2 0.0 collective-permute-done.got_ref
  25.3 1.1 %shard_map.117 = f32[8,64,512]{2,1,0:T(8,128)} custom-call(f32[512,256]{1,0:T(8,128)S(1)} %get-tuple-element.29.feat_ref, f32[512,256]{1,0:T(8,128)S(1)} %shard_map.116.cot_ref, f32[512,512]{1,0:T(8,128)S(1)} %collective-permute-done.got_ref), custom_call_target="tpu_custom_call" | custom-call | flops 100000000 | bytes 2097152 | tf_op jit(solution)/shard_map/pallas_call | solution.py:165
  26.4 24.3 %all_to_all.20.parts_ref = f32[8,64,512]{2,1,0:T(8,128)S(1)} all-to-all(f32[8,64,512]{2,1,0:T(8,128)} %shard_map.117), channel_id=1, replica_groups={{0,16,32,48,64,80,96,112},{8,24,40,56,72,88,104,120},{1,17,33,49,65,81,..., dimensions={0} | all-to-all | bytes 2097152 | tf_op jit(solution)/shard_map/all_to_all | solution.py:630
  50.7 0.1 shard_map.118
  50.8 20.2 %all_to_all.21 = f32[8,64,512]{2,1,0:T(8,128)S(1)} all-to-all(f32[8,64,512]{2,1,0:T(8,128)S(1)} %shard_map.118), channel_id=1, replica_groups={{0,16,32,48,64,80,96,112},{8,24,40,56,72,88,104,120},{1,17,33,49,65,81,..., dimensions={0} | all-to-all | bytes 2097152 | tf_op jit(solution)/shard_map/all_to_all | solution.py:630
  71.1 0.0 collective-permute-start.1
  71.1 2.4 %collective-permute-start.2 = (f32[272,256]{1,0:T(8,128)S(1)}, f32[272,256]{1,0:T(8,128)S(1)}, u32[]{:S(2)}, u32[]{:S(2)}) collective-permute-start(f32[272,256]{1,0:T(8,128)S(1)} %get-tuple-element.41), channel_id=1, source_target_pairs={{0,8},{15,7},{1,9},{14,6},{8,16},{23,15},{9,17},{22,14},{16,24},{3... | collective-permute-start | bytes 835592 | tf_op jit(solution)/shard_map/ppermute | solution.py:657
  73.5 3.6 %shard_map.119 = (f32[256,1024]{1,0:T(8,128)S(1)}, bf16[1024,1024]{1,0:T(8,128)(2,1)S(1)}, f32[128,1024]{1,0:T(8,128)S(1)}) custom-call(f32[512,512]{1,0:T(8,128)S(1)} %bitcast.2, f32[128,1024]{1,0:T(8,128)} %refs_1_.1, bf16[2048,1024]{1,0:T(8,128)(2,1)} %get-tuple-element.30.refs_3_.refs_2_.refs_1_, bf16[2048,1024]{1,0:T(8,128)(2,1)} %get-tuple-element.33.refs_1_.refs_3_.refs_2_), custom_call_target="tpu_custom_call" | custom-call | flops 4000000000 | bytes 9961472 | tf_op jit(solution)/shard_map/pallas_call | solution.py:165
  77.1 0.0 collective-permute-done.1.refs_0_.oth_ref
  77.1 0.0 copy-start
  77.1 3.9 %shard_map.120 = f32[8,256,128]{2,1,0:T(8,128)} custom-call(f32[512,512]{1,0:T(8,128)S(1)} %collective-permute-done.1.refs_0_.oth_ref, f32[128,1024]{1,0:T(8,128)S(1)} %get-tuple-element.38.refs_1_, bf16[2048,1024]{1,0:T(8,128)(2,1)} %get-tuple-element.33.refs_1_.refs_3_.refs_2_, bf16[1024,1024]{1,0:T(8,128)(2,1)S(1)} %get-tuple-element.39.refs_3_, ...), custom_call_target="tpu_custom_call" | custom-call | flops 4000000000 | bytes 8912896 | tf_op jit(solution)/shard_map/pallas_call | solution.py:165
  81.0 0.0 copy-done
  81.0 0.0 copy-start.2
  81.0 0.0 copy-start.3
  81.0 0.0 copy-start.5
  81.1 1.5 %collective-permute-done.2.rim_ref = f32[272,256]{1,0:T(8,128)S(1)} collective-permute-done((f32[272,256]{1,0:T(8,128)S(1)}, f32[272,256]{1,0:T(8,128)S(1)}, u32[]{:S(2)}, u32[]{:S(2)}) %collective-permute-start.2) | collective-permute-done | bytes 278560 | tf_op jit(solution)/shard_map/ppermute | solution.py:657
  82.5 4.2 %all-to-all-start.3 = ((f32[8,256,128]{2,1,0:T(8,128)}), f32[8,256,128]{2,1,0:T(8,128)S(1)}, u32[]{:S(2)}, u32[]{:S(2)}) async-start(f32[8,256,128]{2,1,0:T(8,128)} %shard_map.120), calls=%async_computation.3 | async-start | bytes 2097152 | tf_op jit(solution)/shard_map/all_to_all | solution.py:678
  86.7 0.0 copy-start.1
  86.7 1.2 %copy-done.1 = f32[512,512]{1,0:T(8,128)S(1)} copy-done((f32[512,512]{1,0:T(8,128)S(1)}, f32[512,512]{1,0:T(8,128)}, u32[]{:S(2)}) %copy-start.1) | copy-done | bytes 1048600
  87.9 1.0 shard_map.123
  88.9 0.0 copy-done.2
  88.9 0.0 copy-done.3
  88.9 0.0 copy-done.5
  89.0 0.0 copy-start.4
  89.0 0.9 copy-done.4
  89.9 3.3 %shard_map.121 = (f32[128,128]{1,0:T(8,128)S(1)}, f32[128,128]{1,0:T(8,128)S(1)}) custom-call(f32[272,256]{1,0:T(8,128)S(1)} %collective-permute-done.2.rim_ref, f32[128,1024]{1,0:T(8,128)S(1)} %copy-done.2, f32[3,1024]{1,0:T(4,128)S(1)} %copy-done.3, f32[8,136,128]{2,1,0:T(8,128)S(1)} %all-to-all-done.refs_0_.cot_ref, f32[4,128,128]{2,1,0:T(8,128)S(1)} %copy-done.4, ...), custom_call_target="tpu_custom_call" | custom-call | flops 2000000000 | bytes 1634320 | tf_op jit(solution)/shard_map/pallas_call | solution.py:165
  93.2 7.5 %all-to-all-done.3.parts_ref = f32[8,256,128]{2,1,0:T(8,128)S(1)} async-done(((f32[8,256,128]{2,1,0:T(8,128)}), f32[8,256,128]{2,1,0:T(8,128)S(1)}, u32[]{:S(2)}, u32[]{:S(2)}) %all-to-all-start.3) | async-done | bytes 1048608 | tf_op jit(solution)/shard_map/all_to_all | solution.py:678
  100.7 0.7 shard_map.122
Async XLA Ops:
  3.1 16.1 %all-to-all-start = ((f32[8,136,128]{2,1,0:T(8,128)}), f32[8,136,128]{2,1,0:T(8,128)S(1)}, u32[]{:S(2)}, u32[]{:S(2)}) async-start(f32[8,136,128]{2,1,0:T(8,128)} %get-tuple-element.28.refs_3_), calls=%async_computation | async-start | bytes 1114112 | tf_op jit(solution)/shard_map/all_to_all | solution.py:649
  22.4 2.9 %collective-permute-start = (f32[512,512]{1,0:T(8,128)S(1)}, f32[512,512]{1,0:T(8,128)S(1)}, u32[]{:S(2)}, u32[]{:S(2)}) collective-permute-start(f32[512,512]{1,0:T(8,128)S(1)} %get-tuple-element.35), channel_id=1, source_target_pairs={{0,8},{8,0},{16,24},{24,16},{32,40},{40,32},{48,56},{56,48},{64,72... | collective-permute-start | bytes 3145736 | tf_op jit(solution)/shard_map/ppermute | solution.py:658
  71.1 6.0 %collective-permute-start.1 = (f32[512,512]{1,0:T(8,128)S(1)}, f32[512,512]{1,0:T(8,128)S(1)}, u32[]{:S(2)}, u32[]{:S(2)}) collective-permute-start(f32[512,512]{1,0:T(8,128)S(1)} %bitcast.1), channel_id=1, source_target_pairs={{0,8},{8,0},{16,24},{24,16},{32,40},{40,32},{48,56},{56,48},{64,72... | collective-permute-start | bytes 3145736 | tf_op jit(solution)/shard_map/ppermute | solution.py:671
  71.1 11.5 %collective-permute-start.2 = (f32[272,256]{1,0:T(8,128)S(1)}, f32[272,256]{1,0:T(8,128)S(1)}, u32[]{:S(2)}, u32[]{:S(2)}) collective-permute-start(f32[272,256]{1,0:T(8,128)S(1)} %get-tuple-element.41), channel_id=1, source_target_pairs={{0,8},{15,7},{1,9},{14,6},{8,16},{23,15},{9,17},{22,14},{16,24},{3... | collective-permute-start | bytes 835592 | tf_op jit(solution)/shard_map/ppermute | solution.py:657
  77.1 3.9 %copy-start = (f32[512,512]{1,0:T(8,128)}, f32[512,512]{1,0:T(8,128)S(1)}, u32[]{:S(2)}) copy-start(f32[512,512]{1,0:T(8,128)S(1)} %collective-permute-done.1.refs_0_.oth_ref) | copy-start | bytes 3145732
  81.0 7.9 %copy-start.2 = (f32[128,1024]{1,0:T(8,128)S(1)}, f32[128,1024]{1,0:T(8,128)}, u32[]{:S(2)}) copy-start(f32[128,1024]{1,0:T(8,128)} %feat_ref.1) | copy-start | bytes 1572868
  81.0 7.9 %copy-start.3 = (f32[3,1024]{1,0:T(4,128)S(1)}, f32[3,1024]{1,0:T(4,128)}, u32[]{:S(2)}) copy-start(f32[3,1024]{1,0:T(4,128)} %pos_ref.1) | copy-start | bytes 36868
  81.0 7.9 %copy-start.5 = (f32[4]{0:T(128)S(1)}, f32[4]{0:T(128)}, u32[]{:S(2)}) copy-start(f32[4]{0:T(128)} %rate_ref.1) | copy-start | bytes 52
  82.5 18.1 %all-to-all-start.3 = ((f32[8,256,128]{2,1,0:T(8,128)}), f32[8,256,128]{2,1,0:T(8,128)S(1)}, u32[]{:S(2)}, u32[]{:S(2)}) async-start(f32[8,256,128]{2,1,0:T(8,128)} %shard_map.120), calls=%async_computation.3 | async-start | bytes 2097152 | tf_op jit(solution)/shard_map/all_to_all | solution.py:678
  86.7 1.2 %copy-start.1 = (f32[512,512]{1,0:T(8,128)S(1)}, f32[512,512]{1,0:T(8,128)}, u32[]{:S(2)}) copy-start(f32[512,512]{1,0:T(8,128)} %copy-done) | copy-start | bytes 3145732
  89.0 1.0 copy-start.4
